TPU v7x, 32 devices: a whole 2x2x4 slice. The times are simulated.
32 devices in a mesh: dp: 4 (over z), tile: 8 (over y, x, core).
Axes of the slice: x: 2, y: 2, z: 4, core: 2. Of those that a mesh axis runs over, the one named last changes fastest.
Arguments:
- sensitivity: bfloat16 [2048, 2, 128, 128], P('dp', None, 'tile'), may hold values from -6 to 6
- diffusivity: float32 [2, 128, 128], P(None, 'tile'), may hold values from 0.02 to 0.16
Outputs:
- smoothed: bfloat16 [2048, 2, 128, 128], P('dp', None, 'tile')
- gram_matrix: float32 [2048, 2048], P('dp', 'tile')
All inputs are finite; a program needn't handle non-finite values.
Results may differ from a plain program's by a relative error of at most 0.014.
Values may be sent and summed in bfloat16 or wider, within the bound.
A program may use at most 128 MiB of HBM per device.

v0:
```python
import jax
import jax.numpy as jnp
from jax import lax
from jax.sharding import PartitionSpec as P

STEPS = 4


def extended(block, sides, width):
    for axis, dim in sides:
        count = lax.axis_size(axis)
        forward = [(i, i + 1) for i in range(count - 1)]
        backward = [(target, source) for source, target in forward]
        low = lax.ppermute(
            lax.slice_in_dim(block, block.shape[dim] - width, None, axis=dim), axis, forward
        )
        high = lax.ppermute(lax.slice_in_dim(block, 0, width, axis=dim), axis, backward)
        block = jnp.concatenate([low, block, high], axis=dim)
    return block


def passed_along(value, axis, steps):
    count = lax.axis_size(axis)
    pairs = [(source, (source + steps) % count) for source in range(count)]
    return lax.ppermute(value, axis, pairs)


def relax_step(field, coeff):
    centre = field[:, :, 1:-1]
    coeff_mid = coeff[:, 1:-1]
    change = 0.5 * (coeff_mid + coeff[:, 2:]) * (field[:, :, 2:] - centre)
    change = change + 0.5 * (coeff_mid + coeff[:, :-2]) * (field[:, :, :-2] - centre)
    padded = jnp.pad(centre, ((0, 0), (1, 1), (0, 0), (0, 0)))
    coeff_pad = jnp.pad(coeff_mid, ((1, 1), (0, 0), (0, 0)))
    change = change + 0.5 * (coeff_mid + coeff_pad[2:]) * (padded[:, 2:] - centre)
    change = change + 0.5 * (coeff_mid + coeff_pad[:-2]) * (padded[:, :-2] - centre)
    padded = jnp.pad(centre, ((0, 0), (0, 0), (0, 0), (1, 1)))
    coeff_pad = jnp.pad(coeff_mid, ((0, 0), (0, 0), (1, 1)))
    change = change + 0.5 * (coeff_mid + coeff_pad[:, :, 2:]) * (padded[:, :, :, 2:] - centre)
    change = change + 0.5 * (coeff_mid + coeff_pad[:, :, :-2]) * (padded[:, :, :, :-2] - centre)
    return centre + change


def shards(sensitivity, diffusivity):
    row_count = sensitivity.shape[0]
    width = sensitivity.shape[2]
    coeff_ext = extended(diffusivity, (("tile", 1),), STEPS)
    coeff_near = coeff_ext[:, STEPS - 1 : STEPS + width + 1]
    field = sensitivity
    for step_index in range(STEPS):
        widened = extended(field, (("tile", 2),), 1)
        field = relax_step(widened.astype(jnp.float32), coeff_near).astype(jnp.bfloat16)
    flat_sens = sensitivity.reshape(row_count, -1)
    panel = field.reshape(row_count, -1)
    cycle_len = lax.axis_size("dp")
    cycle_pos = lax.axis_index("dp")
    row_block = jnp.zeros((row_count, row_count * cycle_len), jnp.float32)

    def add_block(block_rows, panel_now, source):
        product = lax.dot_general(
            flat_sens, panel_now, (((1,), (1,)), ((), ())), preferred_element_type=jnp.float32
        )
        column = source * row_count
        return lax.dynamic_update_slice(block_rows, product, (jnp.int32(0), column))

    row_block = add_block(row_block, panel, cycle_pos)

    def one_turn(turn_index, carry):
        block_rows, panel_now = carry
        panel_now = passed_along(panel_now, "dp", 1)
        source = (cycle_pos - turn_index) % cycle_len
        return (add_block(block_rows, panel_now, source), panel_now)

    row_block, panel = lax.fori_loop(1, cycle_len, one_turn, (row_block, panel))
    cell_total = sensitivity.shape[1] * width * sensitivity.shape[3] * lax.axis_size("tile")
    summed = lax.psum(row_block.astype(jnp.bfloat16), "tile").astype(jnp.float32)
    col_count = row_block.shape[1] // lax.axis_size("tile")
    own_cols = lax.dynamic_slice_in_dim(summed, lax.axis_index("tile") * col_count, col_count, 1)
    gram_matrix = own_cols / cell_total
    return (field, gram_matrix)


def solution(mesh):
    in_specs = (P("dp", None, "tile", None), P(None, "tile", None))
    out_specs = (P("dp", None, "tile", None), P("dp", "tile"))
    return jax.shard_map(shards, mesh=mesh, in_specs=in_specs, out_specs=out_specs, check_vma=False)
```

profile of v0, /device:TPU:6, one launch (start us, length us, event | category | flops | bytes accessed | tf_op | source)
XLA Modules:
  0.0 509.1 jit_solution(8160828180584426096)
XLA Ops:
  7.2 3.0 fusion.83
  12.3 3.6 collective-permute-start.2
  18.6 2.4 collective-permute-start.4
  21.0 7.5 %copy.16 = bf16[512,2,16,128]{0,3,2,1:T(8,128)(2,1)} copy(bf16[512,2,16,128]{3,2,1,0:T(8,128)(2,1)} %param.4) | data formatting | bytes 8388608 | tf_op args[0]
  28.9 2.6 maximum_convert_fusion
  33.1 7.6 %fusion.5 = bf16[512,2,16,128]{0,3,2,1:T(8,128)(2,1)S(1)} fusion(f32[512,2,16,128]{0,3,2,1:T(8,128)S(1)} %slice.204, f32[512,2,18,128]{0,3,2,1:T(8,128)S(1)} %maximum_convert_fusion, f32[2,16,128]{2,1,0:T(8,128)S(1)} %get-tuple-element.167, f32[2,16,128]{2,1,0:T(8,128)S(1)} %get-tuple-element.168, f32[2,16,128]{2,1,0:T(8,128)S(1)} %get-tuple-element.165, ...), kind=kLoop, calls=%fused_computation.22 | loop fusion | flops 39845888 | bytes 29458432 | tf_op jit(solution)/shard_map/convert_element_type | solution.py:52
  45.0 3.6 collective-permute-start.6
  48.6 1.9 collective-permute-done.5
  52.7 2.6 maximum_convert_fusion.1
  56.9 7.6 %fusion.13 = bf16[512,2,16,128]{0,3,2,1:T(8,128)(2,1)S(1)} fusion(f32[512,2,16,128]{0,3,2,1:T(8,128)S(1)} %slice.209, f32[512,2,18,128]{0,3,2,1:T(8,128)S(1)} %maximum_convert_fusion.1, f32[2,16,128]{2,1,0:T(8,128)S(1)} %get-tuple-element.167, f32[2,16,128]{2,1,0:T(8,128)S(1)} %get-tuple-element.168, f32[2,16,128]{2,1,0:T(8,128)S(1)} %get-tuple-element.165, ...), kind=kLoop, calls=%fused_computation.30 | loop fusion | flops 39845888 | bytes 29458432 | tf_op jit(solution)/shard_map/convert_element_type | solution.py:52
  68.7 3.8 collective-permute-start.8
  72.6 1.9 collective-permute-done.7
  76.6 2.6 maximum_convert_fusion.2
  80.8 7.6 %fusion.21 = bf16[512,2,16,128]{0,3,2,1:T(8,128)(2,1)S(1)} fusion(f32[512,2,16,128]{0,3,2,1:T(8,128)S(1)} %slice.214, f32[512,2,18,128]{0,3,2,1:T(8,128)S(1)} %maximum_convert_fusion.2, f32[2,16,128]{2,1,0:T(8,128)S(1)} %get-tuple-element.167, f32[2,16,128]{2,1,0:T(8,128)S(1)} %get-tuple-element.168, f32[2,16,128]{2,1,0:T(8,128)S(1)} %get-tuple-element.165, ...), kind=kLoop, calls=%fused_computation.38 | loop fusion | flops 39845888 | bytes 29458432 | tf_op jit(solution)/shard_map/convert_element_type | solution.py:52
  92.7 4.0 collective-permute-start.10
  96.7 8.4 %copy.41 = bf16[64,8,32,128]{3,1,2,0:T(8,128)(2,1)} copy(bf16[64,8,32,128]{3,2,1,0:T(8,128)(2,1)} %bitcast.21) | data formatting | bytes 8388608
  105.4 2.6 maximum_convert_fusion.3
  109.6 7.6 %fusion.29 = bf16[512,2,16,128]{0,3,2,1:T(8,128)(2,1)S(1)} fusion(f32[512,2,16,128]{0,3,2,1:T(8,128)S(1)} %slice.219, f32[512,2,18,128]{0,3,2,1:T(8,128)S(1)} %maximum_convert_fusion.3, f32[2,16,128]{2,1,0:T(8,128)S(1)} %get-tuple-element.167, f32[2,16,128]{2,1,0:T(8,128)S(1)} %get-tuple-element.168, f32[2,16,128]{2,1,0:T(8,128)S(1)} %get-tuple-element.165, ...), kind=kLoop, calls=%fused_computation.46 | loop fusion | flops 39845888 | bytes 29458432 | tf_op jit(solution)/shard_map/convert_element_type | solution.py:52
  119.2 2.3 convolution_bitcast_fusion
  121.7 6.3 %copy.33 = bf16[512,4096]{1,0:T(8,128)(2,1)} copy(bf16[512,4096]{0,1:T(8,128)(2,1)} %bitcast.20) | data formatting | bytes 8388608 | tf_op jit(solution)/shard_map/while | solution.py:74
  128.4 305.0 %while.17 = (s32[]{:T(128)}, bf16[512,2048]{1,0:T(8,128)(2,1)S(1)}, bf16[512,4096]{1,0:T(8,128)(2,1)}, bf16[512,4096]{1,0:T(8,128)(2,1)}, s32[]{:T(128)}, /*inde...) while((s32[]{:T(128)}, bf16[512,2048]{1,0:T(8,128)(2,1)S(1)}, ...), condition=%wide.region_1.2_spmd, body=%wide.region_0.1_spmd.sunk | while | flops 2147483648 | bytes 51380572 | solution.py:74
  130.0 91.7 %collective-permute-done = bf16[512,4096]{1,0:T(8,128)(2,1)} collective-permute-done((bf16[512,4096]{1,0:T(8,128)(2,1)}, bf16[512,4096]{1,0:T(8,128)(2,1)}, u32[]{:S(2)}, u32[]{:S(2)}) %collective-permute-start) | collective-permute-done | bytes 4194336 | tf_op jit(solution)/shard_map/while/body/eval_jaxpr/ppermute | solution.py:25
  221.7 4.7 copy.52
  226.4 4.6 convolution_dynamic-update-slice_fusion.2
  231.1 92.3 %collective-permute-done = bf16[512,4096]{1,0:T(8,128)(2,1)} collective-permute-done((bf16[512,4096]{1,0:T(8,128)(2,1)}, bf16[512,4096]{1,0:T(8,128)(2,1)}, u32[]{:S(2)}, u32[]{:S(2)}) %collective-permute-start) | collective-permute-done | bytes 4194336 | tf_op jit(solution)/shard_map/while/body/eval_jaxpr/ppermute | solution.py:25
  323.4 4.7 copy.52
  328.1 4.6 convolution_dynamic-update-slice_fusion.2
  332.8 91.4 %collective-permute-done = bf16[512,4096]{1,0:T(8,128)(2,1)} collective-permute-done((bf16[512,4096]{1,0:T(8,128)(2,1)}, bf16[512,4096]{1,0:T(8,128)(2,1)}, u32[]{:S(2)}, u32[]{:S(2)}) %collective-permute-start) | collective-permute-done | bytes 4194336 | tf_op jit(solution)/shard_map/while/body/eval_jaxpr/ppermute | solution.py:25
  424.1 4.7 copy.52
  428.8 4.6 convolution_dynamic-update-slice_fusion.2
  434.8 7.8 %copy.34 = bf16[512,2,16,128]{3,2,1,0:T(8,128)(2,1)} copy(bf16[512,2,16,128]{0,3,2,1:T(8,128)(2,1)} %copy-done) | data formatting | bytes 8388608
  442.7 57.8 %all-reduce.12.cloned.1.call-done = bf16[512,2048]{1,0:T(8,128)(2,1)} async-done(((bf16[512,2048]{1,0:T(8,128)(2,1)}), bf16[512,2048]{1,0:T(8,128)(2,1)}) %all-reduce.12.cloned.1.call-update) | async-done | bytes 2097168 | tf_op jit(solution)/shard_map/psum | solution.py:76
  (67 shorter events, 35.9 us)
Async XLA Ops:
  7.2 21.3 %copy-start.7 = (f32[2,16,128]{2,1,0:T(8,128)S(1)}, f32[2,16,128]{2,1,0:T(8,128)}, u32[]{:S(2)}) copy-start(f32[2,16,128]{2,1,0:T(8,128)} %param.5) | copy-start | bytes 49156
  7.2 493.3 %all-reduce.12.cloned.1.call-start = ((), (), s32[]{:S(2)}) async-start(), calls=%async_computation | async-start | bytes 4194304 | tf_op jit(solution)/shard_map/psum | solution.py:76
  10.3 18.3 %collective-permute-start.1 = (bf16[512,2,1,128]{3,0,2,1:T(8,128)(2,1)S(1)}, bf16[512,2,1,128]{3,0,2,1:T(8,128)(2,1)S(1)}, u32[]{:S(2)}, u32[]{:S(2)}) collective-permute-start(bf16[512,2,1,128]{3,0,2,1:T(8,128)(2,1)S(1)} %copy.37), channel_id=1, source_target_pairs={{0,1},{1,2},{2,3},{3,4},{4,5},{5,6},{6,7},{8,9},{9,10},{10,11},{11... | collective-permute-start | bytes 786440 | tf_op jit(solution)/shard_map/ppermute | solution.py:14
  12.3 16.4 %collective-permute-start.2 = (bf16[512,2,1,128]{3,0,2,1:T(8,128)(2,1)S(1)}, bf16[512,2,1,128]{3,0,2,1:T(8,128)(2,1)S(1)}, u32[]{:S(2)}, u32[]{:S(2)}) collective-permute-start(bf16[512,2,1,128]{3,0,2,1:T(8,128)(2,1)S(1)} %copy.38), channel_id=1, source_target_pairs={{1,0},{2,1},{3,2},{4,3},{5,4},{6,5},{7,6},{9,8},{10,9},{11,10},{12... | collective-permute-start | bytes 786440 | tf_op jit(solution)/shard_map/ppermute | solution.py:17
  16.7 11.8 %collective-permute-start.3 = (f32[2,4,128]{2,1,0:T(4,128)S(1)}, f32[2,4,128]{2,1,0:T(4,128)S(1)}, u32[]{:S(2)}, u32[]{:S(2)}) collective-permute-start(f32[2,4,128]{2,1,0:T(4,128)S(1)} %get-tuple-element.169), channel_id=1, source_target_pairs={{1,0},{2,1},{3,2},{4,3},{5,4},{6,5},{7,6},{9,8},{10,9},{11,10},{12... | collective-permute-start | bytes 12296 | tf_op jit(solution)/shard_map/ppermute | solution.py:17
  18.6 9.9 %collective-permute-start.4 = (f32[2,4,128]{2,1,0:T(4,128)S(1)}, f32[2,4,128]{2,1,0:T(4,128)S(1)}, u32[]{:S(2)}, u32[]{:S(2)}) collective-permute-start(f32[2,4,128]{2,1,0:T(4,128)S(1)} %get-tuple-element.170), channel_id=1, source_target_pairs={{0,1},{1,2},{2,3},{3,4},{4,5},{5,6},{6,7},{8,9},{9,10},{10,11},{11... | collective-permute-start | bytes 12296 | tf_op jit(solution)/shard_map/ppermute | solution.py:14
  40.7 1.9 copy-start.2
  42.9 7.7 %collective-permute-start.5 = (bf16[512,2,1,128]{3,0,2,1:T(8,128)(2,1)S(1)}, bf16[512,2,1,128]{3,0,2,1:T(8,128)(2,1)S(1)}, u32[]{:S(2)}, u32[]{:S(2)}) collective-permute-start(bf16[512,2,1,128]{3,0,2,1:T(8,128)(2,1)S(1)} %copy.18), channel_id=1, source_target_pairs={{0,1},{1,2},{2,3},{3,4},{4,5},{5,6},{6,7},{8,9},{9,10},{10,11},{11... | collective-permute-start | bytes 786440 | tf_op jit(solution)/shard_map/ppermute | solution.py:14
  45.0 7.5 %collective-permute-start.6 = (bf16[512,2,1,128]{3,0,2,1:T(8,128)(2,1)S(1)}, bf16[512,2,1,128]{3,0,2,1:T(8,128)(2,1)S(1)}, u32[]{:S(2)}, u32[]{:S(2)}) collective-permute-start(bf16[512,2,1,128]{3,0,2,1:T(8,128)(2,1)S(1)} %copy.19), channel_id=1, source_target_pairs={{1,0},{2,1},{3,2},{4,3},{5,4},{6,5},{7,6},{9,8},{10,9},{11,10},{12... | collective-permute-start | bytes 786440 | tf_op jit(solution)/shard_map/ppermute | solution.py:17
  64.5 1.9 copy-start.3
  66.6 7.9 %collective-permute-start.7 = (bf16[512,2,1,128]{3,0,2,1:T(8,128)(2,1)S(1)}, bf16[512,2,1,128]{3,0,2,1:T(8,128)(2,1)S(1)}, u32[]{:S(2)}, u32[]{:S(2)}) collective-permute-start(bf16[512,2,1,128]{3,0,2,1:T(8,128)(2,1)S(1)} %copy.22), channel_id=1, source_target_pairs={{0,1},{1,2},{2,3},{3,4},{4,5},{5,6},{6,7},{8,9},{9,10},{10,11},{11... | collective-permute-start | bytes 786440 | tf_op jit(solution)/shard_map/ppermute | solution.py:14
  68.7 7.7 %collective-permute-start.8 = (bf16[512,2,1,128]{3,0,2,1:T(8,128)(2,1)S(1)}, bf16[512,2,1,128]{3,0,2,1:T(8,128)(2,1)S(1)}, u32[]{:S(2)}, u32[]{:S(2)}) collective-permute-start(bf16[512,2,1,128]{3,0,2,1:T(8,128)(2,1)S(1)} %copy.23), channel_id=1, source_target_pairs={{1,0},{2,1},{3,2},{4,3},{5,4},{6,5},{7,6},{9,8},{10,9},{11,10},{12... | collective-permute-start | bytes 786440 | tf_op jit(solution)/shard_map/ppermute | solution.py:17
  88.4 1.9 copy-start.1
  90.6 14.5 %collective-permute-start.9 = (bf16[512,2,1,128]{3,0,2,1:T(8,128)(2,1)S(1)}, bf16[512,2,1,128]{3,0,2,1:T(8,128)(2,1)S(1)}, u32[]{:S(2)}, u32[]{:S(2)}) collective-permute-start(bf16[512,2,1,128]{3,0,2,1:T(8,128)(2,1)S(1)} %copy.26), channel_id=1, source_target_pairs={{0,1},{1,2},{2,3},{3,4},{4,5},{5,6},{6,7},{8,9},{9,10},{10,11},{11... | collective-permute-start | bytes 786440 | tf_op jit(solution)/shard_map/ppermute | solution.py:14
  92.7 12.6 %collective-permute-start.10 = (bf16[512,2,1,128]{3,0,2,1:T(8,128)(2,1)S(1)}, bf16[512,2,1,128]{3,0,2,1:T(8,128)(2,1)S(1)}, u32[]{:S(2)}, u32[]{:S(2)}) collective-permute-start(bf16[512,2,1,128]{3,0,2,1:T(8,128)(2,1)S(1)} %copy.27), channel_id=1, source_target_pairs={{1,0},{2,1},{3,2},{4,3},{5,4},{6,5},{7,6},{9,8},{10,9},{11,10},{12... | collective-permute-start | bytes 786440 | tf_op jit(solution)/shard_map/ppermute | solution.py:17
  109.6 9.6 %copy-start.4 = (bf16[512,2,16,128]{0,3,2,1:T(8,128)(2,1)S(1)}, bf16[512,2,16,128]{0,3,2,1:T(8,128)(2,1)}, u32[]{:S(2)}) copy-start(bf16[512,2,16,128]{0,3,2,1:T(8,128)(2,1)} %copy.16) | copy-start | bytes 12582916
  117.2 1.9 copy-start
  128.4 93.3 %collective-permute-start = (bf16[512,4096]{1,0:T(8,128)(2,1)}, bf16[512,4096]{1,0:T(8,128)(2,1)}, u32[]{:S(2)}, u32[]{:S(2)}) collective-permute-start(bf16[512,4096]{1,0:T(8,128)(2,1)} %get-tuple-element.215), channel_id=1, source_target_pairs={{0,8},{8,16},{16,24},{24,0},{1,9},{9,17},{17,25},{25,1},{2,10},{10... | collective-permute-start | bytes 12582920 | tf_op jit(solution)/shard_map/while/body/eval_jaxpr/ppermute | solution.py:25
  130.0 96.4 %copy-start.6 = (bf16[512,4096]{1,0:T(8,128)(2,1)S(1)}, bf16[512,4096]{1,0:T(8,128)(2,1)}, u32[]{:S(2)}) copy-start(bf16[512,4096]{1,0:T(8,128)(2,1)} %get-tuple-element.227) | copy-start | bytes 12582916 | tf_op jit(solution)/shard_map/while
  231.0 92.4 %collective-permute-start = (bf16[512,4096]{1,0:T(8,128)(2,1)}, bf16[512,4096]{1,0:T(8,128)(2,1)}, u32[]{:S(2)}, u32[]{:S(2)}) collective-permute-start(bf16[512,4096]{1,0:T(8,128)(2,1)} %get-tuple-element.215), channel_id=1, source_target_pairs={{0,8},{8,16},{16,24},{24,0},{1,9},{9,17},{17,25},{25,1},{2,10},{10... | collective-permute-start | bytes 12582920 | tf_op jit(solution)/shard_map/while/body/eval_jaxpr/ppermute | solution.py:25
  231.1 97.0 %copy-start.6 = (bf16[512,4096]{1,0:T(8,128)(2,1)S(1)}, bf16[512,4096]{1,0:T(8,128)(2,1)}, u32[]{:S(2)}) copy-start(bf16[512,4096]{1,0:T(8,128)(2,1)} %get-tuple-element.227) | copy-start | bytes 12582916 | tf_op jit(solution)/shard_map/while
  332.7 91.5 %collective-permute-start = (bf16[512,4096]{1,0:T(8,128)(2,1)}, bf16[512,4096]{1,0:T(8,128)(2,1)}, u32[]{:S(2)}, u32[]{:S(2)}) collective-permute-start(bf16[512,4096]{1,0:T(8,128)(2,1)} %get-tuple-element.215), channel_id=1, source_target_pairs={{0,8},{8,16},{16,24},{24,0},{1,9},{9,17},{17,25},{25,1},{2,10},{10... | collective-permute-start | bytes 12582920 | tf_op jit(solution)/shard_map/while/body/eval_jaxpr/ppermute | solution.py:25
  332.8 96.1 %copy-start.6 = (bf16[512,4096]{1,0:T(8,128)(2,1)S(1)}, bf16[512,4096]{1,0:T(8,128)(2,1)}, u32[]{:S(2)}) copy-start(bf16[512,4096]{1,0:T(8,128)(2,1)} %get-tuple-element.227) | copy-start | bytes 12582916 | tf_op jit(solution)/shard_map/while
  433.4 1.4 copy-start.5
Sparse Core Ops, SparseCore 0:
  434.9 65.4 all-reduce.11
where the time goes:
time: 513 us; the launch traced here: 509 us
  waiting for transfers between devices  341 us (66%)
  local copies, waits for them, and re-layouts  66.2 us (13%)
  other arithmetic  42.8 us (8%)
  starting transfers between devices  28.9 us (6%)
  matrix products  16.1 us (3%)
  between operations  14.4 us (3%)
    ppermute x3, waiting for transfers between devices, passed_along(): return lax.ppermute(value, axis, pairs)  275 us
    psum x1, waiting for transfers between devices, shards(): lax.psum(row_block.astype(jnp.bfloat16), 'tile').astype(jnp.float32)  57.8 us
    unnamed x19, local copies, waits for them, and re-layouts  32.9 us
    convert_element_type x4, other arithmetic, shards(): relax_step(widened.astype(jnp.float32), coeff_near).astype(jnp.bfloat16)  30.4 us
    ppermute x5, starting transfers between devices, extended(): lax.ppermute(lax.slice_in_dim(block, 0, width, axis=dim), axis, backward)  17 us
    dot_general x4, matrix products, add_block(): lax.dot_general(flat_sens, panel_now, (((1,), (1,)), ((), ())), preferred...  16.1 us
    while x9, local copies, waits for them, and re-layouts  14.1 us
    convert_element_type x4, other arithmetic, shards(): widened.astype(jnp.float32)  10.5 us
  transfers between devices with their start and end apart: 14, of which 8 were waited for; matrix products, arithmetic and copies ran while one was open for 5% of the time, Pallas kernels for 0%

commit v1 on v0

v1 whole, which is shorter than its diff:
```python
import jax
import jax.numpy as jnp
from jax import lax
from jax.experimental import pallas as pl
from jax.experimental.pallas import tpu as pltpu
from jax.sharding import PartitionSpec as P

STEPS = 4
HALF = 2
MESH = pl.DeviceIdType.MESH
F32 = jnp.float32
BF16 = jnp.bfloat16


def neighbours(block, dim, width, axis="tile"):
    count = lax.axis_size(axis)
    forward = [(i, i + 1) for i in range(count - 1)]
    backward = [(t, s) for s, t in forward]
    low = lax.ppermute(
        lax.slice_in_dim(block, block.shape[dim] - width, None, axis=dim), axis, forward
    )
    high = lax.ppermute(lax.slice_in_dim(block, 0, width, axis=dim), axis, backward)
    return low, high


def extended(block, dim, width):
    low, high = neighbours(block, dim, width)
    return jnp.concatenate([low, block, high], axis=dim)


def coefficients(diffusivity):
    layers, width, ny = diffusivity.shape
    d = extended(diffusivity, 1, HALF)
    tile, tiles = lax.axis_index("tile"), lax.axis_size("tile")
    c = d[:, 1:-1]
    xm = 0.5 * (c + d[:, :-2])
    xp = 0.5 * (c + d[:, 2:])
    cp = jnp.pad(c, ((1, 1), (0, 0), (0, 0)))
    lm = 0.5 * (c + cp[:-2])
    lp = 0.5 * (c + cp[2:])
    cy = jnp.pad(c, ((0, 0), (0, 0), (1, 1)))
    ym = 0.5 * (c + cy[:, :, :-2])
    yp = 0.5 * (c + cy[:, :, 2:])
    a0 = 1.0 - (xm + xp + lm + lp + ym + yp)
    lay = jnp.arange(layers)[:, None, None]
    col = jnp.arange(ny)[None, None, :]
    other = jnp.where(lay == 0, lp, lm)
    ym = jnp.where(col == 0, 0.0, ym)
    yp = jnp.where(col == ny - 1, 0.0, yp)
    x = jnp.arange(width + 2)[None, :, None]
    inside = ((x > 0) | (tile > 0)) & ((x < width + 1) | (tile < tiles - 1))
    stack = jnp.where(inside[None], jnp.stack([a0, xm, xp, other, ym, yp]), 0.0)
    return stack.reshape(6, layers * (width + 2), ny)


def smooth_kernel(width, main_ref, low_ref, high_ref, coeff_ref, out_ref):
    lanes = 128
    ext = width + 2 * HALF

    def load(layer, x):
        if x < HALF:
            at = (layer * HALF + x) * lanes
            return low_ref[:, at : at + lanes].astype(F32)
        if x >= width + HALF:
            at = (layer * HALF + x - width - HALF) * lanes
            return high_ref[:, at : at + lanes].astype(F32)
        at = (layer * width + x - HALF) * lanes
        return main_ref[:, at : at + lanes].astype(F32)

    def step(read, layer, x, cx):
        at = layer * (width + 2) + cx
        w = [coeff_ref[i, at : at + 1, :] for i in range(6)]
        f = read(layer, x)
        total = w[0] * f + w[1] * read(layer, x - 1) + w[2] * read(layer, x + 1)
        total = total + w[3] * read(1 - layer, x)
        total = total + w[4] * pltpu.roll(f, 1, 1)
        return total + w[5] * pltpu.roll(f, lanes - 1, 1)

    first = {}

    def read_first(layer, x):
        if (layer, x) not in first:
            first[layer, x] = step(load, layer, x, x - 1)
        return first[layer, x]

    for x in range(HALF, width + HALF):
        for layer in range(2):
            value = step(read_first, layer, x, x - 1)
            at = (layer * width + x - HALF) * lanes
            out_ref[:, at : at + lanes] = value.astype(BF16)


def two_steps(main, low, high, coeff, width):
    rows, cells = main.shape
    block = 32
    return pl.pallas_call(
        lambda *refs: smooth_kernel(width, *refs),
        out_shape=jax.ShapeDtypeStruct((rows, cells), BF16),
        grid=(rows // block,),
        in_specs=[
            pl.BlockSpec((block, cells), lambda i: (i, 0)),
            pl.BlockSpec((block, low.shape[1]), lambda i: (i, 0)),
            pl.BlockSpec((block, high.shape[1]), lambda i: (i, 0)),
            pl.BlockSpec(coeff.shape, lambda i: (0, 0, 0)),
        ],
        out_specs=pl.BlockSpec((block, cells), lambda i: (i, 0)),
        cost_estimate=pl.CostEstimate(
            flops=rows * cells * 24, bytes_accessed=rows * cells * 8, transcendentals=0
        ),
        name="two_steps",
    )(main, low, high, coeff)


def flat_halo(flat, width):
    rows, cells = flat.shape
    n = width * 128
    w = HALF * 128
    tops = jnp.concatenate([flat[:, n - w : n], flat[:, 2 * n - w :]], axis=1)
    bottoms = jnp.concatenate([flat[:, :w], flat[:, n : n + w]], axis=1)
    count = lax.axis_size("tile")
    forward = [(i, i + 1) for i in range(count - 1)]
    low = lax.ppermute(tops, "tile", forward)
    high = lax.ppermute(bottoms, "tile", [(t, s) for s, t in forward])
    return low, high


def place_kernel(scale, part_ref, out_ref, recv, total, direct_out, turned_out, direct, turned,
                 s1_send, s1_recv, d_send, t_send, d_recv, t_recv):
    p = lax.axis_index("dp")
    t = lax.axis_index("tile")
    tiles = 8
    u, v = t // 2, t % 2
    inner = (p == 1) | (p == 2)
    outer_of = jnp.where(p < 2, 0, 3)
    inner_of = jnp.where(p < 2, 1, 2)
    far_in = 3 - inner_of
    far_out = 3 - outer_of

    barrier = pltpu.get_barrier_semaphore()

    def greet(n, _):
        @pl.when(n != p * tiles + t)
        def _():
            pl.semaphore_signal(barrier, inc=1, device_id=(n // tiles, n % tiles), device_id_type=MESH)
        return 0

    lax.fori_loop(0, 32, greet, 0)
    pl.semaphore_wait(barrier, 31)

    def stage1(s, slot):
        return pltpu.make_async_remote_copy(
            src_ref=part_ref.at[s], dst_ref=recv.at[slot], send_sem=s1_send.at[slot],
            recv_sem=s1_recv.at[slot], device_id=(p, s), device_id_type=MESH)

    for k in range(1, tiles):
        stage1((t + k) % tiles, k - 1).start()
    total[...] = part_ref[t].astype(F32)
    for k in range(1, tiles):
        stage1((t + k) % tiles, k - 1).wait_recv()
        total[...] += recv[k - 1].astype(F32)

    for b in range(6):
        value = total[b] * scale
        direct_out[b] = value.astype(BF16)
        if b < 5:
            turned_out[b] = value.T.astype(BF16)

    rows_of = [outer_of, inner_of, inner_of, outer_of, outer_of, p]
    cols_of = [inner_of, far_in, far_out, far_in, far_out, p]

    def send_direct(b, action):
        dp, dt = rows_of[b], 2 * cols_of[b] + v
        active = inner if b < 5 else (p >= 0)
        mine = (dp == p) & (dt == t)
        where = direct.at[pl.ds(pl.multiple_of(u * 128, 128), 128), :]
        copy = pltpu.make_async_remote_copy(
            src_ref=direct_out.at[b], dst_ref=where, send_sem=d_send.at[b],
            recv_sem=d_recv.at[u], device_id=(dp, dt), device_id_type=MESH)

        @pl.when(active & jnp.logical_not(mine))
        def _():
            copy.start() if action == 0 else copy.wait_send()

        if action == 0:
            @pl.when(active & mine)
            def _():
                where[...] = direct_out[b]

    def send_turned(b, action):
        dp, dt = cols_of[b], 2 * rows_of[b] + u // 2
        mine = (dp == p) & (dt == t)
        col = u % 2
        slot = v * 2 + col
        copy = pltpu.make_async_remote_copy(
            src_ref=turned_out.at[b], dst_ref=turned.at[slot], send_sem=t_send.at[b],
            recv_sem=t_recv.at[slot], device_id=(dp, dt), device_id_type=MESH)

        @pl.when(inner & jnp.logical_not(mine))
        def _():
            copy.start() if action == 0 else copy.wait_send()

        if action == 0:
            @pl.when(inner & mine)
            def _():
                turned[slot] = turned_out[b]

    for b in (4, 2, 3, 1, 0, 5):
        send_direct(b, 0)
        if b < 5:
            send_turned(b, 0)

    g = t // 2
    same_side = (p < 2) == (g < 2)
    cross = jnp.logical_not(same_side)
    has_direct = cross | (p == g) | jnp.logical_not(inner)
    direct_from = jnp.where(p == g, p, inner_of)
    has_turned = cross | ((p != g) & inner)
    turned_from = jnp.where(cross, far_in, inner_of)

    @pl.when(has_direct)
    def _():
        for uu in range(4):
            @pl.when(jnp.logical_not((direct_from == p) & (2 * uu + v == t)))
            def _():
                pltpu.make_async_remote_copy(
                    src_ref=direct_out.at[0], dst_ref=direct.at[pl.ds(uu * 128, 128), :],
                    send_sem=d_send.at[0], recv_sem=d_recv.at[uu], device_id=(p, t),
                    device_id_type=MESH).wait_recv()
        out_ref[...] = direct[...].astype(F32)

    @pl.when(has_turned)
    def _():
        for vv in range(2):
            for cc in range(2):
                @pl.when(jnp.logical_not((turned_from == p) & (2 * (2 * v + cc) + vv == t)))
                def _():
                    pltpu.make_async_remote_copy(
                        src_ref=turned_out.at[0], dst_ref=turned.at[vv * 2 + cc],
                        send_sem=t_send.at[0], recv_sem=t_recv.at[vv * 2 + cc], device_id=(p, t),
                        device_id_type=MESH).wait_recv()

    for vv in range(2):
        for cc in range(2):
            rr, ll = slice(vv * 256, vv * 256 + 256), slice(cc * 128, cc * 128 + 128)

            @pl.when(has_turned & has_direct)
            def _():
                out_ref[rr, ll] += turned[vv * 2 + cc].astype(F32)

            @pl.when(has_turned & jnp.logical_not(has_direct))
            def _():
                out_ref[rr, ll] = turned[vv * 2 + cc].astype(F32)

    for k in range(1, tiles):
        stage1((t + k) % tiles, k - 1).wait_send()
    for b in range(6):
        send_direct(b, 1)
        if b < 5:
            send_turned(b, 1)


def place(part, scale):
    return pl.pallas_call(
        lambda *refs: place_kernel(scale, *refs),
        out_shape=jax.ShapeDtypeStruct((512, 256), F32),
        in_specs=[pl.BlockSpec(memory_space=pltpu.VMEM)],
        out_specs=pl.BlockSpec(memory_space=pltpu.VMEM),
        scratch_shapes=[
            pltpu.VMEM((7, 6, 128, 256), BF16),
            pltpu.VMEM((6, 128, 256), F32),
            pltpu.VMEM((6, 128, 256), BF16),
            pltpu.VMEM((5, 256, 128), BF16),
            pltpu.VMEM((512, 256), BF16),
            pltpu.VMEM((4, 256, 128), BF16),
            pltpu.SemaphoreType.DMA((7,)),
            pltpu.SemaphoreType.DMA((7,)),
            pltpu.SemaphoreType.DMA((6,)),
            pltpu.SemaphoreType.DMA((5,)),
            pltpu.SemaphoreType.DMA((4,)),
            pltpu.SemaphoreType.DMA((4,)),
        ],
        compiler_params=pltpu.CompilerParams(
            collective_id=0, has_side_effects=True, vmem_limit_bytes=32 * 1024 * 1024
        ),
        name="place",
    )(part)


def gram_dot(a, b):
    return lax.dot_general(a, b, (((1,), (1,)), ((), ())), preferred_element_type=F32)


def four_planes(field, total_cells):
    rows, cells = field.shape
    half = cells // 2
    p = lax.axis_index("dp")
    left = p < 2
    first, second = field[:, :half], field[:, half:]
    keep = jnp.where(left, second, first)
    away = jnp.where(left, first, second)
    across = [(1, 2), (2, 1)]
    inward = [(0, 1), (3, 2)]
    far_in = lax.ppermute(away, "dp", across)
    near_away = lax.ppermute(away, "dp", inward)
    near_keep = lax.ppermute(keep, "dp", inward)
    far_out = lax.ppermute(near_away, "dp", across)
    blocks = [
        gram_dot(near_away, away) + gram_dot(near_keep, keep),
        gram_dot(keep, far_in),
        gram_dot(keep, far_out),
        gram_dot(near_keep, far_in),
        gram_dot(near_keep, far_out),
        gram_dot(field, field),
    ]
    cut = [b.astype(BF16).reshape(4, 128, 2, 256).transpose(0, 2, 1, 3).reshape(8, 128, 256) for b in blocks]
    return place(jnp.stack(cut, axis=1), 1.0 / total_cells)


def ring(field, total_cells):
    rows = field.shape[0]
    count = lax.axis_size("dp")
    pos = lax.axis_index("dp")
    pairs = [(s, (s + 1) % count) for s in range(count)]
    block = jnp.zeros((rows, rows * count), F32)

    def add(block, panel, source):
        return lax.dynamic_update_slice(block, gram_dot(field, panel), (jnp.int32(0), source * rows))

    block = add(block, field, pos)

    def turn(i, carry):
        block, panel = carry
        panel = lax.ppermute(panel, "dp", pairs)
        return add(block, panel, (pos - i) % count), panel

    block, _ = lax.fori_loop(1, count, turn, (block, field))
    cols = block.shape[1] // lax.axis_size("tile")
    own = lax.psum_scatter(block.astype(BF16), "tile", scatter_dimension=1, tiled=True)
    return own.astype(F32) / total_cells


def shards(sensitivity, diffusivity):
    rows, layers, width, ny = sensitivity.shape
    total_cells = layers * width * ny * lax.axis_size("tile")
    coeff = coefficients(diffusivity)
    flat = sensitivity.reshape(rows, layers * width * ny)
    middle = two_steps(flat, *flat_halo(flat, width), coeff, width)
    smoothed = two_steps(middle, *flat_halo(middle, width), coeff, width)
    if lax.axis_size("dp") == 4 and lax.axis_size("tile") == 8 and rows == 512:
        gram = four_planes(middle, total_cells)
    else:
        gram = ring(middle, total_cells)
    return smoothed.reshape(sensitivity.shape), gram


def solution(mesh):
    in_specs = (P("dp", None, "tile", None), P(None, "tile", None))
    out_specs = (P("dp", None, "tile", None), P("dp", "tile"))
    return jax.shard_map(shards, mesh=mesh, in_specs=in_specs, out_specs=out_specs, check_vma=False)
```

time: 513 us -> 227 us (0.44)
  the two profiles are of different devices: /device:TPU:6 before, /device:TPU:1 now
where the time goes in v1:
time: 227 us; the launch traced here: 225 us
  Pallas kernels  91.9 us (40%)
  waiting for transfers between devices  45.6 us (20%)
  local copies, waits for them, and re-layouts  28.9 us (13%)
  starting transfers between devices  28.2 us (12%)
  matrix products  23.9 us (11%)
  other arithmetic  5.78 us (3%)
    pallas_call x1, Pallas kernels, place(): pl.pallas_call(lambda *refs: place_kernel(scale, *refs), out_shape=jax.Sh...  57 us
    pallas_call x2, Pallas kernels, two_steps(): pl.pallas_call(lambda *refs: smooth_kernel(width, *refs), out_shape=jax.S...  34.9 us
    ppermute x1, waiting for transfers between devices, four_planes(): near_away = lax.ppermute(away, 'dp', inward)  33.8 us
    dot_general x7, matrix products, gram_dot(): lax.dot_general(a, b, (((1,), (1,)), ((), ())), preferred_element_type=F32)  23.9 us
    unnamed x33, local copies, waits for them, and re-layouts  15.8 us
    reshape x12, local copies, waits for them, and re-layouts, four_planes(): b.astype(BF16).reshape(4, 128, 2, 256).transpose(0, 2, 1, 3)  12.1 us
    ppermute x2, waiting for transfers between devices, flat_halo(): high = lax.ppermute(bottoms, 'tile', [(t, s) for s, t in forward])  8.17 us
    ppermute x2, starting transfers between devices, flat_halo(): low = lax.ppermute(tops, 'tile', forward)  5.91 us
  transfers between devices with their start and end apart: 10, of which 4 were waited for; matrix products, arithmetic and copies ran while one was open for 16% of the time, Pallas kernels for 8%

profile of v1, /device:TPU:1, one launch (start us, length us, event | category | flops | bytes accessed | tf_op | source)
XLA Modules:
  0.0 225.4 jit_solution(3418397114291805410)
XLA Ops:
  1.4 4.5 %collective-permute-start.2 = (f32[2,2,128]{2,1,0:T(2,128)S(1)}, f32[2,2,128]{2,1,0:T(2,128)S(1)}, u32[]{:S(2)}, u32[]{:S(2)}) collective-permute-start(f32[2,2,128]{2,1,0:T(2,128)S(1)} %get-tuple-element.19), channel_id=1, source_target_pairs={{0,1},{1,2},{2,3},{3,4},{4,5},{5,6},{6,7},{8,9},{9,10},{10,11},{11... | collective-permute-start | bytes 6152 | tf_op jit(solution)/shard_map/ppermute | solution.py:19
  5.9 1.9 collective-permute-start.3
  7.8 6.4 %copy.19 = bf16[64,8,32,128]{3,1,2,0:T(8,128)(2,1)S(1)} copy(bf16[64,8,32,128]{3,2,1,0:T(8,128)(2,1)} %bitcast.43) | data formatting | bytes 8388608
  14.3 3.6 %collective-permute-start = (bf16[512,512]{1,0:T(8,128)(2,1)S(1)}, bf16[512,512]{1,0:T(8,128)(2,1)S(1)}, u32[]{:S(2)}, u32[]{:S(2)}) collective-permute-start(bf16[512,512]{1,0:T(8,128)(2,1)S(1)} %pad_maximum_fusion), channel_id=1, source_target_pairs={{0,1},{1,2},{2,3},{3,4},{4,5},{5,6},{6,7},{8,9},{9,10},{10,11},{11... | collective-permute-start | bytes 1572872 | tf_op jit(solution)/shard_map/ppermute | solution.py:122
  18.0 1.9 collective-permute-start.1
  21.1 3.0 %collective-permute-done.refs_1_ = bf16[512,512]{1,0:T(8,128)(2,1)S(1)} collective-permute-done((bf16[512,512]{1,0:T(8,128)(2,1)S(1)}, bf16[512,512]{1,0:T(8,128)(2,1)S(1)}, u32[]{:S(2)}, u32[]{:S(2)}) %collective-permute-start) | collective-permute-done | bytes 524320 | tf_op jit(solution)/shard_map/ppermute | solution.py:122
  24.1 8.2 %collective-permute-done.1.refs_2_ = bf16[512,512]{1,0:T(8,128)(2,1)S(1)} collective-permute-done((bf16[512,512]{1,0:T(8,128)(2,1)S(1)}, bf16[512,512]{1,0:T(8,128)(2,1)S(1)}, u32[]{:S(2)}, u32[]{:S(2)}) %collective-permute-start.1) | collective-permute-done | bytes 524320 | tf_op jit(solution)/shard_map/ppermute | solution.py:123
  33.0 17.3 %two_steps.2.refs_0_ = bf16[512,4096]{1,0:T(8,128)(2,1)} custom-call(bf16[512,4096]{1,0:T(8,128)(2,1)} %bitcast.41, bf16[512,512]{1,0:T(8,128)(2,1)} %copy-done.7, bf16[512,512]{1,0:T(8,128)(2,1)} %copy-done.8, f32[6,36,128]{2,1,0:T(8,128)} %broadcast_select_fusion.2.refs_3_), custom_call_target="tpu_custom_call" | custom-call | flops 50331648 | bytes 16777216 | tf_op jit(solution)/shard_map/two_steps/pallas_call | solution.py:96
  50.4 4.0 %broadcast_select_fusion.1 = (bf16[512,2048]{1,0:T(8,128)(2,1)}, bf16[512,2048]{1,0:T(8,128)(2,1)S(1)}) fusion(pred[]{:T(512)S(6)} %lt.17, bf16[512,4096]{1,0:T(8,128)(2,1)} %two_steps.2.refs_0_), kind=kLoop, calls=%fused_computation.2 | loop fusion | flops 2097152 | bytes 8388609 | tf_op jit(solution)/shard_map/jit(_where)/select_n | solution.py:300
  54.3 4.5 %collective-permute-start.6 = (bf16[512,2048]{1,0:T(8,128)(2,1)}, bf16[512,2048]{1,0:T(8,128)(2,1)}, u32[]{:S(2)}, u32[]{:S(2)}) collective-permute-start(bf16[512,2048]{1,0:T(8,128)(2,1)} %get-tuple-element.2), channel_id=1, source_target_pairs={{0,8},{24,16},{1,9},{25,17},{2,10},{26,18},{3,11},{27,19},{4,12},{... | collective-permute-start | bytes 6291464 | tf_op jit(solution)/shard_map/ppermute | solution.py:304
  58.8 2.0 collective-permute-start.8
  60.8 2.7 %collective-permute-start.7 = (bf16[512,2048]{1,0:T(8,128)(2,1)S(1)}, bf16[512,2048]{1,0:T(8,128)(2,1)}, u32[]{:S(2)}, u32[]{:S(2)}) collective-permute-start(bf16[512,2048]{1,0:T(8,128)(2,1)S(1)} %get-tuple-element.3), channel_id=1, source_target_pairs={{0,8},{24,16},{1,9},{25,17},{2,10},{26,18},{3,11},{27,19},{4,12},{... | collective-permute-start | bytes 6291464 | tf_op jit(solution)/shard_map/ppermute | solution.py:305
  63.6 2.3 %collective-permute-start.4 = (bf16[512,512]{1,0:T(8,128)(2,1)S(1)}, bf16[512,512]{1,0:T(8,128)(2,1)}, u32[]{:S(2)}, u32[]{:S(2)}) collective-permute-start(bf16[512,512]{1,0:T(8,128)(2,1)S(1)} %pad_maximum_fusion.2), channel_id=1, source_target_pairs={{0,1},{1,2},{2,3},{3,4},{4,5},{5,6},{6,7},{8,9},{9,10},{10,11},{11... | collective-permute-start | bytes 1572872 | tf_op jit(solution)/shard_map/ppermute | solution.py:122
  66.7 2.8 %collective-permute-start.5 = (bf16[512,512]{1,0:T(8,128)(2,1)}, bf16[512,512]{1,0:T(8,128)(2,1)}, u32[]{:S(2)}, u32[]{:S(2)}) collective-permute-start(bf16[512,512]{1,0:T(8,128)(2,1)} %pad_maximum_fusion.3), channel_id=1, source_target_pairs={{1,0},{2,1},{3,2},{4,3},{5,4},{6,5},{7,6},{9,8},{10,9},{11,10},{12... | collective-permute-start | bytes 1572872 | tf_op jit(solution)/shard_map/ppermute | solution.py:123
  69.6 33.8 %collective-permute-done.6 = bf16[512,2048]{1,0:T(8,128)(2,1)} collective-permute-done((bf16[512,2048]{1,0:T(8,128)(2,1)}, bf16[512,2048]{1,0:T(8,128)(2,1)}, u32[]{:S(2)}, u32[]{:S(2)}) %collective-permute-start.6) | collective-permute-done | bytes 2097184 | tf_op jit(solution)/shard_map/ppermute | solution.py:304
  103.3 2.0 collective-permute-start.9
  105.3 3.2 %convolution_convert_fusion = bf16[512,512]{1,0:T(8,128)(2,1)} fusion(bf16[512,4096]{1,0:T(8,128)(2,1)S(1)} %copy-done), kind=kOutput, calls=%fused_computation.4 | convolution fusion | flops 2147745792 | bytes 4718592 | tf_op jit(solution)/shard_map/dot_general | solution.py:290
  108.5 1.2 reshape.80
  110.5 17.6 %two_steps.3 = bf16[512,4096]{1,0:T(8,128)(2,1)} custom-call(bf16[512,4096]{1,0:T(8,128)(2,1)} %two_steps.2.refs_0_, bf16[512,512]{1,0:T(8,128)(2,1)} %collective-permute-done.4.refs_1_, bf16[512,512]{1,0:T(8,128)(2,1)} %collective-permute-done.5.refs_2_, f32[6,36,128]{2,1,0:T(8,128)} %broadcast_select_fusion.2.refs_3_), custom_call_target="tpu_custom_call" | custom-call | flops 50331648 | bytes 16777216 | tf_op jit(solution)/shard_map/two_steps/pallas_call | solution.py:96
  128.1 5.5 %copy.17 = bf16[64,8,32,128]{3,2,1,0:T(8,128)(2,1)} copy(bf16[64,8,32,128]{3,1,2,0:T(8,128)(2,1)} %bitcast.42) | data formatting | bytes 8388608
  133.6 2.9 %convolution_convert_fusion.4 = bf16[512,512]{1,0:T(8,128)(2,1)S(1)} fusion(bf16[512,2048]{1,0:T(8,128)(2,1)S(1)} %get-tuple-element.3, bf16[512,2048]{1,0:T(8,128)(2,1)} %collective-permute-done.8), kind=kOutput, calls=%fused_computation.8 | convolution fusion | flops 1074003968 | bytes 4718592 | tf_op jit(solution)/shard_map/dot_general | solution.py:290
  138.2 2.9 %fusion.14 = f32[512,512]{1,0:T(8,128)S(1)} fusion(bf16[512,2048]{1,0:T(8,128)(2,1)} %collective-permute-done.7, bf16[512,2048]{1,0:T(8,128)(2,1)S(1)} %get-tuple-element.3), kind=kOutput, calls=%fused_computation.56 | convolution fusion | flops 1073741824 | bytes 5242880 | tf_op jit(solution)/shard_map/dot_general | solution.py:290
  141.1 3.5 %fusion = bf16[512,512]{1,0:T(8,128)(2,1)S(1)} fusion(f32[512,512]{1,0:T(8,128)S(1)} %fusion.14, bf16[512,2048]{1,0:T(8,128)(2,1)} %collective-permute-done.6, bf16[512,2048]{1,0:T(8,128)(2,1)} %get-tuple-element.2), kind=kOutput, calls=%fused_computation.9 | convolution fusion | flops 1074266112 | bytes 5767168 | tf_op jit(solution)/shard_map/dot_general | solution.py:290
  145.6 3.5 %convolution_convert_fusion.2 = bf16[512,512]{1,0:T(8,128)(2,1)S(1)} fusion(bf16[512,2048]{1,0:T(8,128)(2,1)} %collective-permute-done.7, bf16[512,2048]{1,0:T(8,128)(2,1)} %collective-permute-done.8), kind=kOutput, calls=%fused_computation.6 | convolution fusion | flops 1074003968 | bytes 4718592 | tf_op jit(solution)/shard_map/dot_general | solution.py:290
  150.1 1.2 constant_dynamic-update-slice_fusion.11
  151.3 3.7 %convolution_convert_fusion.3 = bf16[512,512]{1,0:T(8,128)(2,1)} fusion(bf16[512,2048]{1,0:T(8,128)(2,1)S(1)} %copy-done.6, bf16[512,2048]{1,0:T(8,128)(2,1)} %collective-permute-done.9), kind=kOutput, calls=%fused_computation.7 | convolution fusion | flops 1074003968 | bytes 4718592 | tf_op jit(solution)/shard_map/dot_general | solution.py:290
  155.0 2.0 reshape.77
  157.0 1.9 copy.12
  158.9 4.3 %convolution_convert_fusion.1 = bf16[512,512]{1,0:T(8,128)(2,1)} fusion(bf16[512,2048]{1,0:T(8,128)(2,1)} %collective-permute-done.7, bf16[512,2048]{1,0:T(8,128)(2,1)} %collective-permute-done.9), kind=kOutput, calls=%fused_computation.5 | convolution fusion | flops 1074003968 | bytes 4718592 | tf_op jit(solution)/shard_map/dot_general | solution.py:290
  163.2 2.0 reshape.79
  165.2 1.2 copy.14
  167.6 57.0 %place.1 = f32[512,256]{1,0:T(8,128)S(1)} custom-call(bf16[8,6,128,256]{3,2,1,0:T(8,128)(2,1)S(1)} %constant_dynamic-update-slice_fusion.6.refs_0_), custom_call_target="tpu_custom_call" | custom-call | tf_op jit(solution)/shard_map/place/pallas_call | solution.py:263
  (67 shorter events, 10.3 us)
Async XLA Ops:
  1.4 18.7 %collective-permute-start.2 = (f32[2,2,128]{2,1,0:T(2,128)S(1)}, f32[2,2,128]{2,1,0:T(2,128)S(1)}, u32[]{:S(2)}, u32[]{:S(2)}) collective-permute-start(f32[2,2,128]{2,1,0:T(2,128)S(1)} %get-tuple-element.19), channel_id=1, source_target_pairs={{0,1},{1,2},{2,3},{3,4},{4,5},{5,6},{6,7},{8,9},{9,10},{10,11},{11... | collective-permute-start | bytes 6152 | tf_op jit(solution)/shard_map/ppermute | solution.py:19
  5.9 14.2 %collective-permute-start.3 = (f32[2,2,128]{2,1,0:T(2,128)S(1)}, f32[2,2,128]{2,1,0:T(2,128)S(1)}, u32[]{:S(2)}, u32[]{:S(2)}) collective-permute-start(f32[2,2,128]{2,1,0:T(2,128)S(1)} %get-tuple-element.20), channel_id=1, source_target_pairs={{1,0},{2,1},{3,2},{4,3},{5,4},{6,5},{7,6},{9,8},{10,9},{11,10},{12... | collective-permute-start | bytes 6152 | tf_op jit(solution)/shard_map/ppermute | solution.py:22
  14.1 3.9 %copy-start.1 = (bf16[64,8,32,128]{3,1,2,0:T(8,128)(2,1)}, bf16[64,8,32,128]{3,1,2,0:T(8,128)(2,1)S(1)}, u32[]{:S(2)}) copy-start(bf16[64,8,32,128]{3,1,2,0:T(8,128)(2,1)S(1)} %copy.19) | copy-start | bytes 12582916
  14.2 5.9 %copy-start.9 = (f32[2,16,128]{2,1,0:T(8,128)S(1)}, f32[2,16,128]{2,1,0:T(8,128)}, u32[]{:S(2)}) copy-start(f32[2,16,128]{2,1,0:T(8,128)} %param.3) | copy-start | bytes 49156
  14.3 9.8 %collective-permute-start = (bf16[512,512]{1,0:T(8,128)(2,1)S(1)}, bf16[512,512]{1,0:T(8,128)(2,1)S(1)}, u32[]{:S(2)}, u32[]{:S(2)}) collective-permute-start(bf16[512,512]{1,0:T(8,128)(2,1)S(1)} %pad_maximum_fusion), channel_id=1, source_target_pairs={{0,1},{1,2},{2,3},{3,4},{4,5},{5,6},{6,7},{8,9},{9,10},{10,11},{11... | collective-permute-start | bytes 1572872 | tf_op jit(solution)/shard_map/ppermute | solution.py:122
  18.0 14.2 %collective-permute-start.1 = (bf16[512,512]{1,0:T(8,128)(2,1)S(1)}, bf16[512,512]{1,0:T(8,128)(2,1)S(1)}, u32[]{:S(2)}, u32[]{:S(2)}) collective-permute-start(bf16[512,512]{1,0:T(8,128)(2,1)S(1)} %pad_maximum_fusion.1), channel_id=1, source_target_pairs={{1,0},{2,1},{3,2},{4,3},{5,4},{6,5},{7,6},{9,8},{10,9},{11,10},{12... | collective-permute-start | bytes 1572872 | tf_op jit(solution)/shard_map/ppermute | solution.py:123
  24.1 8.2 %copy-start.7 = (bf16[512,512]{1,0:T(8,128)(2,1)}, bf16[512,512]{1,0:T(8,128)(2,1)S(1)}, u32[]{:S(2)}) copy-start(bf16[512,512]{1,0:T(8,128)(2,1)S(1)} %collective-permute-done.refs_1_) | copy-start | bytes 1572868
  32.2 0.8 copy-start.8
  50.4 13.1 %copy-start = (bf16[512,4096]{1,0:T(8,128)(2,1)S(1)}, bf16[512,4096]{1,0:T(8,128)(2,1)}, u32[]{:S(2)}) copy-start(bf16[512,4096]{1,0:T(8,128)(2,1)} %two_steps.2.refs_0_) | copy-start | bytes 12582916
  54.3 83.8 %copy-start.5 = (bf16[512,2048]{1,0:T(8,128)(2,1)}, bf16[512,2048]{1,0:T(8,128)(2,1)S(1)}, u32[]{:S(2)}) copy-start(bf16[512,2048]{1,0:T(8,128)(2,1)S(1)} %get-tuple-element.3) | copy-start | bytes 6291460
  54.3 49.0 %collective-permute-start.6 = (bf16[512,2048]{1,0:T(8,128)(2,1)}, bf16[512,2048]{1,0:T(8,128)(2,1)}, u32[]{:S(2)}, u32[]{:S(2)}) collective-permute-start(bf16[512,2048]{1,0:T(8,128)(2,1)} %get-tuple-element.2), channel_id=1, source_target_pairs={{0,8},{24,16},{1,9},{25,17},{2,10},{26,18},{3,11},{27,19},{4,12},{... | collective-permute-start | bytes 6291464 | tf_op jit(solution)/shard_map/ppermute | solution.py:304
  58.8 74.7 %collective-permute-start.8 = (bf16[512,2048]{1,0:T(8,128)(2,1)}, bf16[512,2048]{1,0:T(8,128)(2,1)}, u32[]{:S(2)}, u32[]{:S(2)}) collective-permute-start(bf16[512,2048]{1,0:T(8,128)(2,1)} %get-tuple-element.2), channel_id=1, source_target_pairs={{8,16},{16,8},{9,17},{17,9},{10,18},{18,10},{11,19},{19,11},{12,20... | collective-permute-start | bytes 6291464 | tf_op jit(solution)/shard_map/ppermute | solution.py:303
  60.8 77.4 %collective-permute-start.7 = (bf16[512,2048]{1,0:T(8,128)(2,1)S(1)}, bf16[512,2048]{1,0:T(8,128)(2,1)}, u32[]{:S(2)}, u32[]{:S(2)}) collective-permute-start(bf16[512,2048]{1,0:T(8,128)(2,1)S(1)} %get-tuple-element.3), channel_id=1, source_target_pairs={{0,8},{24,16},{1,9},{25,17},{2,10},{26,18},{3,11},{27,19},{4,12},{... | collective-permute-start | bytes 6291464 | tf_op jit(solution)/shard_map/ppermute | solution.py:305
  63.6 46.9 %collective-permute-start.4 = (bf16[512,512]{1,0:T(8,128)(2,1)S(1)}, bf16[512,512]{1,0:T(8,128)(2,1)}, u32[]{:S(2)}, u32[]{:S(2)}) collective-permute-start(bf16[512,512]{1,0:T(8,128)(2,1)S(1)} %pad_maximum_fusion.2), channel_id=1, source_target_pairs={{0,1},{1,2},{2,3},{3,4},{4,5},{5,6},{6,7},{8,9},{9,10},{10,11},{11... | collective-permute-start | bytes 1572872 | tf_op jit(solution)/shard_map/ppermute | solution.py:122
  66.7 43.8 %collective-permute-start.5 = (bf16[512,512]{1,0:T(8,128)(2,1)}, bf16[512,512]{1,0:T(8,128)(2,1)}, u32[]{:S(2)}, u32[]{:S(2)}) collective-permute-start(bf16[512,512]{1,0:T(8,128)(2,1)} %pad_maximum_fusion.3), channel_id=1, source_target_pairs={{1,0},{2,1},{3,2},{4,3},{5,4},{6,5},{7,6},{9,8},{10,9},{11,10},{12... | collective-permute-start | bytes 1572872 | tf_op jit(solution)/shard_map/ppermute | solution.py:123
  103.3 48.0 %collective-permute-start.9 = (bf16[512,2048]{1,0:T(8,128)(2,1)}, bf16[512,2048]{1,0:T(8,128)(2,1)}, u32[]{:S(2)}, u32[]{:S(2)}) collective-permute-start(bf16[512,2048]{1,0:T(8,128)(2,1)} %collective-permute-done.6), channel_id=1, source_target_pairs={{8,16},{16,8},{9,17},{17,9},{10,18},{18,10},{11,19},{19,11},{12,20... | collective-permute-start | bytes 6291464 | tf_op jit(solution)/shard_map/ppermute | solution.py:306
  149.2 2.1 copy-start.4
  149.2 2.1 copy-start.6
  165.2 2.3 %copy-start.3 = (bf16[4,128,2,256]{3,1,2,0:T(8,128)(2,1)S(1)}, bf16[4,128,2,256]{3,1,2,0:T(8,128)(2,1)}, u32[]{:S(2)}) copy-start(bf16[4,128,2,256]{3,1,2,0:T(8,128)(2,1)} %copy.13) | copy-start | bytes 1572868
  165.2 2.4 %copy-start.2 = (bf16[4,128,2,256]{3,1,2,0:T(8,128)(2,1)S(1)}, bf16[4,128,2,256]{3,1,2,0:T(8,128)(2,1)}, u32[]{:S(2)}) copy-start(bf16[4,128,2,256]{3,1,2,0:T(8,128)(2,1)} %copy.15) | copy-start | bytes 1572868

commit v2 on v1

--- a/solution.py
+++ b/solution.py
@@ -53,9 +53,9 @@
     return stack.reshape(6, layers * (width + 2), ny)
 
 
-def smooth_kernel(width, main_ref, low_ref, high_ref, coeff_ref, out_ref):
+def smooth_kernel(width, split, main_ref, low_ref, high_ref, coeff_ref, out_ref, *halves):
     lanes = 128
-    ext = width + 2 * HALF
+    half = width * lanes
 
     def load(layer, x):
         if x < HALF:
@@ -88,14 +88,28 @@
             value = step(read_first, layer, x, x - 1)
             at = (layer * width + x - HALF) * lanes
             out_ref[:, at : at + lanes] = value.astype(BF16)
-
-
-def two_steps(main, low, high, coeff, width):
+    if split:
+        away_ref, keep_ref = halves
+        left = 2 * lax.axis_index("dp") < lax.axis_size("dp")
+
+        @pl.when(left)
+        def _():
+            away_ref[...] = out_ref[:, :half]
+            keep_ref[...] = out_ref[:, half:]
+
+        @pl.when(jnp.logical_not(left))
+        def _():
+            away_ref[...] = out_ref[:, half:]
+            keep_ref[...] = out_ref[:, :half]
+
+
+def two_steps(main, low, high, coeff, width, split):
     rows, cells = main.shape
     block = 32
+    outs = [cells] + ([cells // 2] * 2 if split else [])
     return pl.pallas_call(
-        lambda *refs: smooth_kernel(width, *refs),
-        out_shape=jax.ShapeDtypeStruct((rows, cells), BF16),
+        lambda *refs: smooth_kernel(width, split, *refs),
+        out_shape=[jax.ShapeDtypeStruct((rows, n), BF16) for n in outs],
         grid=(rows // block,),
         in_specs=[
             pl.BlockSpec((block, cells), lambda i: (i, 0)),
@@ -103,7 +117,7 @@
             pl.BlockSpec((block, high.shape[1]), lambda i: (i, 0)),
             pl.BlockSpec(coeff.shape, lambda i: (0, 0, 0)),
         ],
-        out_specs=pl.BlockSpec((block, cells), lambda i: (i, 0)),
+        out_specs=[pl.BlockSpec((block, n), lambda i: (i, 0)) for n in outs],
         cost_estimate=pl.CostEstimate(
             flops=rows * cells * 24, bytes_accessed=rows * cells * 8, transcendentals=0
         ),
@@ -111,12 +125,7 @@
     )(main, low, high, coeff)
 
 
-def flat_halo(flat, width):
-    rows, cells = flat.shape
-    n = width * 128
-    w = HALF * 128
-    tops = jnp.concatenate([flat[:, n - w : n], flat[:, 2 * n - w :]], axis=1)
-    bottoms = jnp.concatenate([flat[:, :w], flat[:, n : n + w]], axis=1)
+def exchange(tops, bottoms):
     count = lax.axis_size("tile")
     forward = [(i, i + 1) for i in range(count - 1)]
     low = lax.ppermute(tops, "tile", forward)
@@ -124,8 +133,25 @@
     return low, high
 
 
-def place_kernel(scale, part_ref, out_ref, recv, total, direct_out, turned_out, direct, turned,
-                 s1_send, s1_recv, d_send, t_send, d_recv, t_recv):
+def flat_halo(flat, width):
+    n = width * 128
+    w = HALF * 128
+    tops = jnp.concatenate([flat[:, n - w : n], flat[:, 2 * n - w :]], axis=1)
+    bottoms = jnp.concatenate([flat[:, :w], flat[:, n : n + w]], axis=1)
+    return exchange(tops, bottoms)
+
+
+def first_halo(block):
+    rows, width = block.shape[0], block.shape[2]
+    return exchange(
+        block[:, :, width - HALF :].reshape(rows, -1), block[:, :, :HALF].reshape(rows, -1)
+    )
+
+
+def place_kernel(scale, *refs):
+    blocks, out_ref = refs[:6], refs[6]
+    (partner, half_out, quarter, direct_out, turned_out, direct, turned,
+     s1_send, s1_recv, s2_send, s2_recv, d_send, t_send, d_recv, t_recv) = refs[7:]
     p = lax.axis_index("dp")
     t = lax.axis_index("tile")
     tiles = 8
@@ -147,23 +173,27 @@
     lax.fori_loop(0, 32, greet, 0)
     pl.semaphore_wait(barrier, 31)
 
-    def stage1(s, slot):
+    def when_active(b, run):
+        if b == 5:
+            run()
+        else:
+            pl.when(inner)(run)
+
+    own_cols = pl.ds(pl.multiple_of(v * 256, 256), 256)
+    other_cols = pl.ds(pl.multiple_of((1 - v) * 256, 256), 256)
+    own_rows = pl.ds(pl.multiple_of(u * 128, 128), 128)
+
+    def stage1(b):
         return pltpu.make_async_remote_copy(
-            src_ref=part_ref.at[s], dst_ref=recv.at[slot], send_sem=s1_send.at[slot],
-            recv_sem=s1_recv.at[slot], device_id=(p, s), device_id_type=MESH)
-
-    for k in range(1, tiles):
-        stage1((t + k) % tiles, k - 1).start()
-    total[...] = part_ref[t].astype(F32)
-    for k in range(1, tiles):
-        stage1((t + k) % tiles, k - 1).wait_recv()
-        total[...] += recv[k - 1].astype(F32)
-
-    for b in range(6):
-        value = total[b] * scale
-        direct_out[b] = value.astype(BF16)
-        if b < 5:
-            turned_out[b] = value.T.astype(BF16)
+            src_ref=blocks[b].at[:, other_cols], dst_ref=partner.at[b], send_sem=s1_send.at[b],
+            recv_sem=s1_recv.at[b], device_id=(p, 2 * u + 1 - v), device_id_type=MESH)
+
+    def stage2(b, k):
+        to = (u + k) % 4
+        return pltpu.make_async_remote_copy(
+            src_ref=half_out.at[b, pl.ds(pl.multiple_of(to * 128, 128), 128), :],
+            dst_ref=quarter.at[b, k - 1], send_sem=s2_send.at[b, k - 1],
+            recv_sem=s2_recv.at[b, k - 1], device_id=(p, 2 * to + v), device_id_type=MESH)
 
     rows_of = [outer_of, inner_of, inner_of, outer_of, outer_of, p]
     cols_of = [inner_of, far_in, far_out, far_in, far_out, p]
@@ -204,7 +234,27 @@
             def _():
                 turned[slot] = turned_out[b]
 
-    for b in (4, 2, 3, 1, 0, 5):
+    order = (1, 3, 0, 2, 4, 5)
+    for b in order:
+        when_active(b, lambda b=b: stage1(b).start())
+    for b in order:
+        def add_partner(b=b):
+            stage1(b).wait_recv()
+            half_out[b] = (blocks[b][:, own_cols].astype(F32) + partner[b].astype(F32)).astype(BF16)
+            for k in range(1, 4):
+                stage2(b, k).start()
+        when_active(b, add_partner)
+    for b in order:
+        def finish(b=b):
+            value = blocks[b][own_rows, own_cols].astype(F32) + partner[b, own_rows, :].astype(F32)
+            for k in range(1, 4):
+                stage2(b, k).wait_recv()
+                value = value + quarter[b, k - 1].astype(F32)
+            value = value * scale
+            direct_out[b] = value.astype(BF16)
+            if b < 5:
+                turned_out[b] = value.T.astype(BF16)
+        when_active(b, finish)
         send_direct(b, 0)
         if b < 5:
             send_turned(b, 0)
@@ -251,29 +301,35 @@
             def _():
                 out_ref[rr, ll] = turned[vv * 2 + cc].astype(F32)
 
-    for k in range(1, tiles):
-        stage1((t + k) % tiles, k - 1).wait_send()
     for b in range(6):
+        def sent(b=b):
+            stage1(b).wait_send()
+            for k in range(1, 4):
+                stage2(b, k).wait_send()
+        when_active(b, sent)
         send_direct(b, 1)
         if b < 5:
             send_turned(b, 1)
 
 
-def place(part, scale):
+def place(blocks, scale):
     return pl.pallas_call(
         lambda *refs: place_kernel(scale, *refs),
         out_shape=jax.ShapeDtypeStruct((512, 256), F32),
-        in_specs=[pl.BlockSpec(memory_space=pltpu.VMEM)],
+        in_specs=[pl.BlockSpec(memory_space=pltpu.VMEM)] * 6,
         out_specs=pl.BlockSpec(memory_space=pltpu.VMEM),
         scratch_shapes=[
-            pltpu.VMEM((7, 6, 128, 256), BF16),
-            pltpu.VMEM((6, 128, 256), F32),
+            pltpu.VMEM((6, 512, 256), BF16),
+            pltpu.VMEM((6, 512, 256), BF16),
+            pltpu.VMEM((6, 3, 128, 256), BF16),
             pltpu.VMEM((6, 128, 256), BF16),
             pltpu.VMEM((5, 256, 128), BF16),
             pltpu.VMEM((512, 256), BF16),
             pltpu.VMEM((4, 256, 128), BF16),
-            pltpu.SemaphoreType.DMA((7,)),
-            pltpu.SemaphoreType.DMA((7,)),
+            pltpu.SemaphoreType.DMA((6,)),
+            pltpu.SemaphoreType.DMA((6,)),
+            pltpu.SemaphoreType.DMA((6, 3)),
+            pltpu.SemaphoreType.DMA((6, 3)),
             pltpu.SemaphoreType.DMA((6,)),
             pltpu.SemaphoreType.DMA((5,)),
             pltpu.SemaphoreType.DMA((4,)),
@@ -283,21 +339,14 @@
             collective_id=0, has_side_effects=True, vmem_limit_bytes=32 * 1024 * 1024
         ),
         name="place",
-    )(part)
+    )(*blocks)
 
 
 def gram_dot(a, b):
     return lax.dot_general(a, b, (((1,), (1,)), ((), ())), preferred_element_type=F32)
 
 
-def four_planes(field, total_cells):
-    rows, cells = field.shape
-    half = cells // 2
-    p = lax.axis_index("dp")
-    left = p < 2
-    first, second = field[:, :half], field[:, half:]
-    keep = jnp.where(left, second, first)
-    away = jnp.where(left, first, second)
+def four_planes(away, keep, total_cells):
     across = [(1, 2), (2, 1)]
     inward = [(0, 1), (3, 2)]
     far_in = lax.ppermute(away, "dp", across)
@@ -310,10 +359,9 @@
         gram_dot(keep, far_out),
         gram_dot(near_keep, far_in),
         gram_dot(near_keep, far_out),
-        gram_dot(field, field),
+        gram_dot(away, away) + gram_dot(keep, keep),
     ]
-    cut = [b.astype(BF16).reshape(4, 128, 2, 256).transpose(0, 2, 1, 3).reshape(8, 128, 256) for b in blocks]
-    return place(jnp.stack(cut, axis=1), 1.0 / total_cells)
+    return place([b.astype(BF16) for b in blocks], 1.0 / total_cells)
 
 
 def ring(field, total_cells):
@@ -344,10 +392,11 @@
     total_cells = layers * width * ny * lax.axis_size("tile")
     coeff = coefficients(diffusivity)
     flat = sensitivity.reshape(rows, layers * width * ny)
-    middle = two_steps(flat, *flat_halo(flat, width), coeff, width)
-    smoothed = two_steps(middle, *flat_halo(middle, width), coeff, width)
-    if lax.axis_size("dp") == 4 and lax.axis_size("tile") == 8 and rows == 512:
-        gram = four_planes(middle, total_cells)
+    planes = lax.axis_size("dp") == 4 and lax.axis_size("tile") == 8 and rows == 512
+    middle, *halves = two_steps(flat, *first_halo(sensitivity), coeff, width, planes)
+    (smoothed,) = two_steps(middle, *flat_halo(middle, width), coeff, width, False)
+    if planes:
+        gram = four_planes(*halves, total_cells)
     else:
         gram = ring(middle, total_cells)
     return smoothed.reshape(sensitivity.shape), gram

time: 227 us -> 193 us (0.85)
  the two profiles are of different devices: /device:TPU:1 before, /device:TPU:6 now
where the time goes in v2:
time: 193 us; the launch traced here: 190 us
  Pallas kernels  69.1 us (36%)
  waiting for transfers between devices  47.4 us (25%)
  starting transfers between devices  26.9 us (14%)
  local copies, waits for them, and re-layouts  23.9 us (12%)
  matrix products  21.2 us (11%)
    pallas_call x2, Pallas kernels, two_steps(): pl.pallas_call(lambda *refs: smooth_kernel(width, split, *refs), out_shap...  35.6 us
    pallas_call x1, Pallas kernels, place(): pl.pallas_call(lambda *refs: place_kernel(scale, *refs), out_shape=jax.Sh...  33.4 us
    ppermute x1, waiting for transfers between devices, four_planes(): near_away = lax.ppermute(away, 'dp', inward)  32 us
    dot_general x8, matrix products, gram_dot(): lax.dot_general(a, b, (((1,), (1,)), ((), ())), preferred_element_type=F32)  21.2 us
    unnamed x28, local copies, waits for them, and re-layouts  18.8 us
    ppermute x1, waiting for transfers between devices, four_planes(): near_keep = lax.ppermute(keep, 'dp', inward)  15.4 us
    ppermute x2, starting transfers between devices, exchange(): high = lax.ppermute(bottoms, 'tile', [(t, s) for s, t in forward])  7.42 us
    ppermute x1, starting transfers between devices, four_planes(): near_away = lax.ppermute(away, 'dp', inward)  4.79 us
  transfers between devices with their start and end apart: 10, of which 2 were waited for; matrix products, arithmetic and copies ran while one was open for 17% of the time, Pallas kernels for 9%

profile of v2, /device:TPU:6, one launch (start us, length us, event | category | flops | bytes accessed | tf_op | source)
XLA Modules:
  0.0 190.5 jit_solution(14164738380850103882)
XLA Ops:
  0.6 3.0 %fusion.13 = (bf16[512,2,2,128]{3,2,1,0:T(2,128)(2,1)S(1)}, bf16[512,2,2,128]{3,2,1,0:T(2,128)(2,1)S(1)}) fusion(bf16[512,2,16,128]{3,2,1,0:T(8,128)(2,1)} %param.2), kind=kLoop, calls=%fused_computation.45 | loop fusion | bytes 2097152 | tf_op jit(solution)/shard_map/slice | solution.py:147
  4.7 1.9 %collective-permute-start = (bf16[512,512]{1,0:T(8,128)(2,1)S(1)}, bf16[512,512]{1,0:T(8,128)(2,1)S(1)}, u32[]{:S(2)}, u32[]{:S(2)}) collective-permute-start(bf16[512,512]{1,0:T(8,128)(2,1)S(1)} %copy.5), channel_id=1, source_target_pairs={{0,1},{1,2},{2,3},{3,4},{4,5},{5,6},{6,7},{8,9},{9,10},{10,11},{11... | collective-permute-start | bytes 1572872 | tf_op jit(solution)/shard_map/ppermute | solution.py:131
  6.6 0.7 copy.9
  7.5 3.6 %collective-permute-start.1 = (bf16[512,512]{1,0:T(8,128)(2,1)S(1)}, bf16[512,512]{1,0:T(8,128)(2,1)S(1)}, u32[]{:S(2)}, u32[]{:S(2)}) collective-permute-start(bf16[512,512]{1,0:T(8,128)(2,1)S(1)} %copy.7), channel_id=1, source_target_pairs={{1,0},{2,1},{3,2},{4,3},{5,4},{6,5},{7,6},{9,8},{10,9},{11,10},{12... | collective-permute-start | bytes 1572872 | tf_op jit(solution)/shard_map/ppermute | solution.py:132
  11.2 1.9 %collective-permute-start.3 = (f32[2,2,128]{2,1,0:T(2,128)S(1)}, f32[2,2,128]{2,1,0:T(2,128)S(1)}, u32[]{:S(2)}, u32[]{:S(2)}) collective-permute-start(f32[2,2,128]{2,1,0:T(2,128)S(1)} %get-tuple-element.22), channel_id=1, source_target_pairs={{1,0},{2,1},{3,2},{4,3},{5,4},{6,5},{7,6},{9,8},{10,9},{11,10},{12... | collective-permute-start | bytes 6152 | tf_op jit(solution)/shard_map/ppermute | solution.py:22
  13.1 2.4 %collective-permute-start.2 = (f32[2,2,128]{2,1,0:T(2,128)S(1)}, f32[2,2,128]{2,1,0:T(2,128)S(1)}, u32[]{:S(2)}, u32[]{:S(2)}) collective-permute-start(f32[2,2,128]{2,1,0:T(2,128)S(1)} %get-tuple-element.21), channel_id=1, source_target_pairs={{0,1},{1,2},{2,3},{3,4},{4,5},{5,6},{6,7},{8,9},{9,10},{10,11},{11... | collective-permute-start | bytes 6152 | tf_op jit(solution)/shard_map/ppermute | solution.py:19
  15.6 8.4 %copy.13 = bf16[64,8,32,128]{3,1,2,0:T(8,128)(2,1)} copy(bf16[64,8,32,128]{3,2,1,0:T(8,128)(2,1)} %bitcast.28) | data formatting | bytes 8388608
  25.1 0.8 copy-done
  26.0 18.3 %two_steps.2 = (bf16[512,4096]{1,0:T(8,128)(2,1)}, bf16[512,2048]{1,0:T(8,128)(2,1)}, bf16[512,2048]{1,0:T(8,128)(2,1)}) custom-call(bf16[512,4096]{1,0:T(8,128)(2,1)} %bitcast.26, bf16[512,512]{1,0:T(8,128)(2,1)} %copy-done, bf16[512,512]{1,0:T(8,128)(2,1)} %copy-done.1, f32[6,36,128]{2,1,0:T(8,128)} %broadcast_select_fusion.refs_3_), custom_call_target="tpu_custom_call" | custom-call | flops 50331648 | bytes 16777216 | tf_op jit(solution)/shard_map/two_steps/pallas_call | solution.py:110
  44.3 4.8 %collective-permute-start.6 = (bf16[512,2048]{1,0:T(8,128)(2,1)}, bf16[512,2048]{1,0:T(8,128)(2,1)}, u32[]{:S(2)}, u32[]{:S(2)}) collective-permute-start(bf16[512,2048]{1,0:T(8,128)(2,1)} %get-tuple-element.6), channel_id=1, source_target_pairs={{0,8},{24,16},{1,9},{25,17},{2,10},{26,18},{3,11},{27,19},{4,12},{... | collective-permute-start | bytes 6291464 | tf_op jit(solution)/shard_map/ppermute | solution.py:353
  49.1 2.6 %collective-permute-start.7 = (bf16[512,2048]{1,0:T(8,128)(2,1)}, bf16[512,2048]{1,0:T(8,128)(2,1)}, u32[]{:S(2)}, u32[]{:S(2)}) collective-permute-start(bf16[512,2048]{1,0:T(8,128)(2,1)} %get-tuple-element.7), channel_id=1, source_target_pairs={{0,8},{24,16},{1,9},{25,17},{2,10},{26,18},{3,11},{27,19},{4,12},{... | collective-permute-start | bytes 6291464 | tf_op jit(solution)/shard_map/ppermute | solution.py:354
  51.7 2.0 %collective-permute-start.8 = (bf16[512,2048]{1,0:T(8,128)(2,1)}, bf16[512,2048]{1,0:T(8,128)(2,1)}, u32[]{:S(2)}, u32[]{:S(2)}) collective-permute-start(bf16[512,2048]{1,0:T(8,128)(2,1)} %get-tuple-element.6), channel_id=1, source_target_pairs={{8,16},{16,8},{9,17},{17,9},{10,18},{18,10},{11,19},{19,11},{12,20... | collective-permute-start | bytes 6291464 | tf_op jit(solution)/shard_map/ppermute | solution.py:352
  53.7 1.4 fusion.12
  55.1 1.9 %collective-permute-start.4 = (bf16[512,512]{1,0:T(8,128)(2,1)S(1)}, bf16[512,512]{1,0:T(8,128)(2,1)S(1)}, u32[]{:S(2)}, u32[]{:S(2)}) collective-permute-start(bf16[512,512]{1,0:T(8,128)(2,1)S(1)} %pad_maximum_fusion), channel_id=1, source_target_pairs={{0,1},{1,2},{2,3},{3,4},{4,5},{5,6},{6,7},{8,9},{9,10},{10,11},{11... | collective-permute-start | bytes 1572872 | tf_op jit(solution)/shard_map/ppermute | solution.py:131
  57.1 3.8 %collective-permute-start.5 = (bf16[512,512]{1,0:T(8,128)(2,1)S(1)}, bf16[512,512]{1,0:T(8,128)(2,1)S(1)}, u32[]{:S(2)}, u32[]{:S(2)}) collective-permute-start(bf16[512,512]{1,0:T(8,128)(2,1)S(1)} %pad_maximum_fusion.1), channel_id=1, source_target_pairs={{1,0},{2,1},{3,2},{4,3},{5,4},{6,5},{7,6},{9,8},{10,9},{11,10},{12... | collective-permute-start | bytes 1572872 | tf_op jit(solution)/shard_map/ppermute | solution.py:132
  60.9 1.3 fusion.16
  62.2 32.0 %collective-permute-done.6 = bf16[512,2048]{1,0:T(8,128)(2,1)} collective-permute-done((bf16[512,2048]{1,0:T(8,128)(2,1)}, bf16[512,2048]{1,0:T(8,128)(2,1)}, u32[]{:S(2)}, u32[]{:S(2)}) %collective-permute-start.6) | collective-permute-done | bytes 2097184 | tf_op jit(solution)/shard_map/ppermute | solution.py:353
  94.2 2.0 %collective-permute-start.9 = (bf16[512,2048]{1,0:T(8,128)(2,1)}, bf16[512,2048]{1,0:T(8,128)(2,1)}, u32[]{:S(2)}, u32[]{:S(2)}) collective-permute-start(bf16[512,2048]{1,0:T(8,128)(2,1)} %collective-permute-done.6), channel_id=1, source_target_pairs={{8,16},{16,8},{9,17},{17,9},{10,18},{18,10},{11,19},{19,11},{12,20... | collective-permute-start | bytes 6291464 | tf_op jit(solution)/shard_map/ppermute | solution.py:355
  96.2 1.3 fusion.1.refs_5_
  97.5 0.8 copy-done.2
  98.3 0.8 copy-done.3
  99.1 17.4 %two_steps.3 = bf16[512,4096]{1,0:T(8,128)(2,1)} custom-call(bf16[512,4096]{1,0:T(8,128)(2,1)} %get-tuple-element.5.refs_0_, bf16[512,512]{1,0:T(8,128)(2,1)} %copy-done.2, bf16[512,512]{1,0:T(8,128)(2,1)} %copy-done.3, f32[6,36,128]{2,1,0:T(8,128)} %broadcast_select_fusion.refs_3_), custom_call_target="tpu_custom_call" | custom-call | flops 50331648 | bytes 16777216 | tf_op jit(solution)/shard_map/two_steps/pallas_call | solution.py:110
  116.4 5.6 %copy.11 = bf16[64,8,32,128]{3,2,1,0:T(8,128)(2,1)} copy(bf16[64,8,32,128]{3,1,2,0:T(8,128)(2,1)} %bitcast.27) | data formatting | bytes 8388608
  122.1 15.4 %collective-permute-done.7 = bf16[512,2048]{1,0:T(8,128)(2,1)} collective-permute-done((bf16[512,2048]{1,0:T(8,128)(2,1)}, bf16[512,2048]{1,0:T(8,128)(2,1)}, u32[]{:S(2)}, u32[]{:S(2)}) %collective-permute-start.7) | collective-permute-done | bytes 2097184 | tf_op jit(solution)/shard_map/ppermute | solution.py:354
  137.5 2.9 %fusion.15 = f32[512,512]{1,0:T(8,128)S(1)} fusion(bf16[512,2048]{1,0:T(8,128)(2,1)} %collective-permute-done.7, bf16[512,2048]{1,0:T(8,128)(2,1)S(1)} %copy-done.6), kind=kOutput, calls=%fused_computation.47 | convolution fusion | flops 1073741824 | bytes 5242880 | tf_op jit(solution)/shard_map/dot_general | solution.py:346
  140.4 2.9 %convolution_convert_fusion.3.refs_1_ = bf16[512,512]{1,0:T(8,128)(2,1)S(1)} fusion(bf16[512,2048]{1,0:T(8,128)(2,1)S(1)} %copy-done.6, bf16[512,2048]{1,0:T(8,128)(2,1)} %collective-permute-done.8), kind=kOutput, calls=%fused_computation.6 | convolution fusion | flops 1074003968 | bytes 4718592 | tf_op jit(solution)/shard_map/dot_general | solution.py:346
  143.3 3.7 %convolution_convert_fusion.1.refs_3_ = bf16[512,512]{1,0:T(8,128)(2,1)S(1)} fusion(bf16[512,2048]{1,0:T(8,128)(2,1)} %collective-permute-done.7, bf16[512,2048]{1,0:T(8,128)(2,1)} %collective-permute-done.8), kind=kOutput, calls=%fused_computation.4 | convolution fusion | flops 1074003968 | bytes 4718592 | tf_op jit(solution)/shard_map/dot_general | solution.py:346
  146.9 2.9 %fusion.refs_0_ = bf16[512,512]{1,0:T(8,128)(2,1)S(1)} fusion(f32[512,512]{1,0:T(8,128)S(1)} %fusion.15, bf16[512,2048]{1,0:T(8,128)(2,1)} %collective-permute-done.6, bf16[512,2048]{1,0:T(8,128)(2,1)S(1)} %copy-done.8), kind=kOutput, calls=%fused_computation.7 | convolution fusion | flops 1074266112 | bytes 5767168 | tf_op jit(solution)/shard_map/dot_general | solution.py:346
  149.8 2.9 %convolution_convert_fusion.2.refs_2_ = bf16[512,512]{1,0:T(8,128)(2,1)S(1)} fusion(bf16[512,2048]{1,0:T(8,128)(2,1)S(1)} %copy-done.6, bf16[512,2048]{1,0:T(8,128)(2,1)} %collective-permute-done.9), kind=kOutput, calls=%fused_computation.5 | convolution fusion | flops 1074003968 | bytes 4718592 | tf_op jit(solution)/shard_map/dot_general | solution.py:346
  152.7 3.5 %convolution_convert_fusion.refs_4_ = bf16[512,512]{1,0:T(8,128)(2,1)S(1)} fusion(bf16[512,2048]{1,0:T(8,128)(2,1)} %collective-permute-done.7, bf16[512,2048]{1,0:T(8,128)(2,1)} %collective-permute-done.9), kind=kOutput, calls=%fused_computation.3 | convolution fusion | flops 1074003968 | bytes 4718592 | tf_op jit(solution)/shard_map/dot_general | solution.py:346
  156.2 33.4 %place.1 = f32[512,256]{1,0:T(8,128)S(1)} custom-call(bf16[512,512]{1,0:T(8,128)(2,1)S(1)} %fusion.refs_0_, bf16[512,512]{1,0:T(8,128)(2,1)S(1)} %convolution_convert_fusion.3.refs_1_, bf16[512,512]{1,0:T(8,128)(2,1)S(1)} %convolution_convert_fusion.2.refs_2_, bf16[512,512]{1,0:T(8,128)(2,1)S(1)} %convolution_convert_fusion.1.refs_3_, ...), custom_call_target="tpu_custom_call" | custom-call | tf_op jit(solution)/shard_map/place/pallas_call | solution.py:316
  189.7 0.8 copy.20
  (49 shorter events, 2.5 us)
Async XLA Ops:
  3.7 7.5 %copy-start.4 = (f32[2,16,128]{2,1,0:T(8,128)S(1)}, f32[2,16,128]{2,1,0:T(8,128)}, u32[]{:S(2)}) copy-start(f32[2,16,128]{2,1,0:T(8,128)} %param.3) | copy-start | bytes 49156
  4.7 20.4 %collective-permute-start = (bf16[512,512]{1,0:T(8,128)(2,1)S(1)}, bf16[512,512]{1,0:T(8,128)(2,1)S(1)}, u32[]{:S(2)}, u32[]{:S(2)}) collective-permute-start(bf16[512,512]{1,0:T(8,128)(2,1)S(1)} %copy.5), channel_id=1, source_target_pairs={{0,1},{1,2},{2,3},{3,4},{4,5},{5,6},{6,7},{8,9},{9,10},{10,11},{11... | collective-permute-start | bytes 1572872 | tf_op jit(solution)/shard_map/ppermute | solution.py:131
  7.5 17.5 %collective-permute-start.1 = (bf16[512,512]{1,0:T(8,128)(2,1)S(1)}, bf16[512,512]{1,0:T(8,128)(2,1)S(1)}, u32[]{:S(2)}, u32[]{:S(2)}) collective-permute-start(bf16[512,512]{1,0:T(8,128)(2,1)S(1)} %copy.7), channel_id=1, source_target_pairs={{1,0},{2,1},{3,2},{4,3},{5,4},{6,5},{7,6},{9,8},{10,9},{11,10},{12... | collective-permute-start | bytes 1572872 | tf_op jit(solution)/shard_map/ppermute | solution.py:132
  11.2 12.8 %collective-permute-start.3 = (f32[2,2,128]{2,1,0:T(2,128)S(1)}, f32[2,2,128]{2,1,0:T(2,128)S(1)}, u32[]{:S(2)}, u32[]{:S(2)}) collective-permute-start(f32[2,2,128]{2,1,0:T(2,128)S(1)} %get-tuple-element.22), channel_id=1, source_target_pairs={{1,0},{2,1},{3,2},{4,3},{5,4},{6,5},{7,6},{9,8},{10,9},{11,10},{12... | collective-permute-start | bytes 6152 | tf_op jit(solution)/shard_map/ppermute | solution.py:22
  13.1 10.9 %collective-permute-start.2 = (f32[2,2,128]{2,1,0:T(2,128)S(1)}, f32[2,2,128]{2,1,0:T(2,128)S(1)}, u32[]{:S(2)}, u32[]{:S(2)}) collective-permute-start(f32[2,2,128]{2,1,0:T(2,128)S(1)} %get-tuple-element.21), channel_id=1, source_target_pairs={{0,1},{1,2},{2,3},{3,4},{4,5},{5,6},{6,7},{8,9},{9,10},{10,11},{11... | collective-permute-start | bytes 6152 | tf_op jit(solution)/shard_map/ppermute | solution.py:19
  25.1 0.8 copy-start
  25.1 1.0 copy-start.1
  44.3 49.9 %collective-permute-start.6 = (bf16[512,2048]{1,0:T(8,128)(2,1)}, bf16[512,2048]{1,0:T(8,128)(2,1)}, u32[]{:S(2)}, u32[]{:S(2)}) collective-permute-start(bf16[512,2048]{1,0:T(8,128)(2,1)} %get-tuple-element.6), channel_id=1, source_target_pairs={{0,8},{24,16},{1,9},{25,17},{2,10},{26,18},{3,11},{27,19},{4,12},{... | collective-permute-start | bytes 6291464 | tf_op jit(solution)/shard_map/ppermute | solution.py:353
  49.1 88.4 %collective-permute-start.7 = (bf16[512,2048]{1,0:T(8,128)(2,1)}, bf16[512,2048]{1,0:T(8,128)(2,1)}, u32[]{:S(2)}, u32[]{:S(2)}) collective-permute-start(bf16[512,2048]{1,0:T(8,128)(2,1)} %get-tuple-element.7), channel_id=1, source_target_pairs={{0,8},{24,16},{1,9},{25,17},{2,10},{26,18},{3,11},{27,19},{4,12},{... | collective-permute-start | bytes 6291464 | tf_op jit(solution)/shard_map/ppermute | solution.py:354
  51.7 88.7 %collective-permute-start.8 = (bf16[512,2048]{1,0:T(8,128)(2,1)}, bf16[512,2048]{1,0:T(8,128)(2,1)}, u32[]{:S(2)}, u32[]{:S(2)}) collective-permute-start(bf16[512,2048]{1,0:T(8,128)(2,1)} %get-tuple-element.6), channel_id=1, source_target_pairs={{8,16},{16,8},{9,17},{17,9},{10,18},{18,10},{11,19},{19,11},{12,20... | collective-permute-start | bytes 6291464 | tf_op jit(solution)/shard_map/ppermute | solution.py:352
  53.7 7.2 %copy-start.5 = (bf16[512,2048]{1,0:T(8,128)(2,1)S(1)}, bf16[512,2048]{1,0:T(8,128)(2,1)}, u32[]{:S(2)}) copy-start(bf16[512,2048]{1,0:T(8,128)(2,1)} %get-tuple-element.7) | copy-start | bytes 6291460
  55.1 42.3 %collective-permute-start.4 = (bf16[512,512]{1,0:T(8,128)(2,1)S(1)}, bf16[512,512]{1,0:T(8,128)(2,1)S(1)}, u32[]{:S(2)}, u32[]{:S(2)}) collective-permute-start(bf16[512,512]{1,0:T(8,128)(2,1)S(1)} %pad_maximum_fusion), channel_id=1, source_target_pairs={{0,1},{1,2},{2,3},{3,4},{4,5},{5,6},{6,7},{8,9},{9,10},{10,11},{11... | collective-permute-start | bytes 1572872 | tf_op jit(solution)/shard_map/ppermute | solution.py:131
  57.1 39.1 %copy-start.7 = (bf16[512,2048]{1,0:T(8,128)(2,1)S(1)}, bf16[512,2048]{1,0:T(8,128)(2,1)}, u32[]{:S(2)}) copy-start(bf16[512,2048]{1,0:T(8,128)(2,1)} %get-tuple-element.6) | copy-start | bytes 6291460
  57.1 40.4 %collective-permute-start.5 = (bf16[512,512]{1,0:T(8,128)(2,1)S(1)}, bf16[512,512]{1,0:T(8,128)(2,1)S(1)}, u32[]{:S(2)}, u32[]{:S(2)}) collective-permute-start(bf16[512,512]{1,0:T(8,128)(2,1)S(1)} %pad_maximum_fusion.1), channel_id=1, source_target_pairs={{1,0},{2,1},{3,2},{4,3},{5,4},{6,5},{7,6},{9,8},{10,9},{11,10},{12... | collective-permute-start | bytes 1572872 | tf_op jit(solution)/shard_map/ppermute | solution.py:132
  94.2 55.6 %collective-permute-start.9 = (bf16[512,2048]{1,0:T(8,128)(2,1)}, bf16[512,2048]{1,0:T(8,128)(2,1)}, u32[]{:S(2)}, u32[]{:S(2)}) collective-permute-start(bf16[512,2048]{1,0:T(8,128)(2,1)} %collective-permute-done.6), channel_id=1, source_target_pairs={{8,16},{16,8},{9,17},{17,9},{10,18},{18,10},{11,19},{19,11},{12,20... | collective-permute-start | bytes 6291464 | tf_op jit(solution)/shard_map/ppermute | solution.py:355
  97.5 0.8 copy-start.2
  98.3 0.8 copy-start.3
  116.4 21.0 %copy-start.6 = (bf16[512,2048]{1,0:T(8,128)(2,1)S(1)}, bf16[512,2048]{1,0:T(8,128)(2,1)}, u32[]{:S(2)}) copy-start(bf16[512,2048]{1,0:T(8,128)(2,1)} %get-tuple-element.7) | copy-start | bytes 6291460
  143.3 3.7 %copy-start.8 = (bf16[512,2048]{1,0:T(8,128)(2,1)S(1)}, bf16[512,2048]{1,0:T(8,128)(2,1)}, u32[]{:S(2)}) copy-start(bf16[512,2048]{1,0:T(8,128)(2,1)} %get-tuple-element.6) | copy-start | bytes 6291460

commit v3 on v2

--- a/solution.py
+++ b/solution.py
@@ -148,10 +148,24 @@
     )
 
 
-def place_kernel(scale, *refs):
-    blocks, out_ref = refs[:6], refs[6]
-    (partner, half_out, quarter, direct_out, turned_out, direct, turned,
-     s1_send, s1_recv, s2_send, s2_recv, d_send, t_send, d_recv, t_recv) = refs[7:]
+def place_kernel(scale, late, *refs):
+    order = (3, 0, 2, 4) if late else (1, 5)
+    slot_of = {b: n for n, b in enumerate(order)}
+    if late:
+        near_ref, far_in_ref, far_out_ref, keep_ref, begun_ref, early_ref = refs[:6]
+        refs = refs[6:]
+    else:
+        block_refs, refs = refs[:2], refs[2:]
+    (out_ref, outgoing, own, partner, half_out, quarter, direct_out, turned_out, direct, turned,
+     s1_send, s1_recv, s2_send, s2_recv, d_send, t_send, d_recv, t_recv) = refs
+
+    def product(b, cols):
+        if not late:
+            return block_refs[slot_of[b]][:, cols].astype(F32)
+        rows_ref = keep_ref if b == 2 else near_ref
+        cols_ref = {0: keep_ref, 2: far_out_ref, 3: far_in_ref, 4: far_out_ref}[b]
+        value = gram_dot(rows_ref[...], cols_ref[cols, :])
+        return value + begun_ref[:, cols] if b == 0 else value
     p = lax.axis_index("dp")
     t = lax.axis_index("tile")
     tiles = 8
@@ -184,16 +198,18 @@
     own_rows = pl.ds(pl.multiple_of(u * 128, 128), 128)
 
     def stage1(b):
+        n = slot_of[b]
         return pltpu.make_async_remote_copy(
-            src_ref=blocks[b].at[:, other_cols], dst_ref=partner.at[b], send_sem=s1_send.at[b],
-            recv_sem=s1_recv.at[b], device_id=(p, 2 * u + 1 - v), device_id_type=MESH)
+            src_ref=outgoing.at[n], dst_ref=partner.at[n], send_sem=s1_send.at[n],
+            recv_sem=s1_recv.at[n], device_id=(p, 2 * u + 1 - v), device_id_type=MESH)
 
     def stage2(b, k):
+        n = slot_of[b]
         to = (u + k) % 4
         return pltpu.make_async_remote_copy(
-            src_ref=half_out.at[b, pl.ds(pl.multiple_of(to * 128, 128), 128), :],
-            dst_ref=quarter.at[b, k - 1], send_sem=s2_send.at[b, k - 1],
-            recv_sem=s2_recv.at[b, k - 1], device_id=(p, 2 * to + v), device_id_type=MESH)
+            src_ref=half_out.at[n, pl.ds(pl.multiple_of(to * 128, 128), 128), :],
+            dst_ref=quarter.at[n, k - 1], send_sem=s2_send.at[n, k - 1],
+            recv_sem=s2_recv.at[n, k - 1], device_id=(p, 2 * to + v), device_id_type=MESH)
 
     rows_of = [outer_of, inner_of, inner_of, outer_of, outer_of, p]
     cols_of = [inner_of, far_in, far_out, far_in, far_out, p]
@@ -204,7 +220,7 @@
         mine = (dp == p) & (dt == t)
         where = direct.at[pl.ds(pl.multiple_of(u * 128, 128), 128), :]
         copy = pltpu.make_async_remote_copy(
-            src_ref=direct_out.at[b], dst_ref=where, send_sem=d_send.at[b],
+            src_ref=direct_out.at[slot_of[b]], dst_ref=where, send_sem=d_send.at[slot_of[b]],
             recv_sem=d_recv.at[u], device_id=(dp, dt), device_id_type=MESH)
 
         @pl.when(active & jnp.logical_not(mine))
@@ -214,7 +230,7 @@
         if action == 0:
             @pl.when(active & mine)
             def _():
-                where[...] = direct_out[b]
+                where[...] = direct_out[slot_of[b]]
 
     def send_turned(b, action):
         dp, dt = cols_of[b], 2 * rows_of[b] + u // 2
@@ -222,7 +238,7 @@
         col = u % 2
         slot = v * 2 + col
         copy = pltpu.make_async_remote_copy(
-            src_ref=turned_out.at[b], dst_ref=turned.at[slot], send_sem=t_send.at[b],
+            src_ref=turned_out.at[slot_of[b]], dst_ref=turned.at[slot], send_sem=t_send.at[slot_of[b]],
             recv_sem=t_recv.at[slot], device_id=(dp, dt), device_id_type=MESH)
 
         @pl.when(inner & jnp.logical_not(mine))
@@ -232,28 +248,33 @@
         if action == 0:
             @pl.when(inner & mine)
             def _():
-                turned[slot] = turned_out[b]
-
-    order = (1, 3, 0, 2, 4, 5)
+                turned[slot] = turned_out[slot_of[b]]
+
     for b in order:
-        when_active(b, lambda b=b: stage1(b).start())
+        def begin(b=b):
+            outgoing[slot_of[b]] = product(b, other_cols).astype(BF16)
+            stage1(b).start()
+        when_active(b, begin)
     for b in order:
         def add_partner(b=b):
+            n = slot_of[b]
+            own[n] = product(b, own_cols)
             stage1(b).wait_recv()
-            half_out[b] = (blocks[b][:, own_cols].astype(F32) + partner[b].astype(F32)).astype(BF16)
+            half_out[n] = (own[n] + partner[n].astype(F32)).astype(BF16)
             for k in range(1, 4):
                 stage2(b, k).start()
         when_active(b, add_partner)
     for b in order:
         def finish(b=b):
-            value = blocks[b][own_rows, own_cols].astype(F32) + partner[b, own_rows, :].astype(F32)
+            n = slot_of[b]
+            value = own[n, own_rows, :] + partner[n, own_rows, :].astype(F32)
             for k in range(1, 4):
                 stage2(b, k).wait_recv()
-                value = value + quarter[b, k - 1].astype(F32)
+                value = value + quarter[n, k - 1].astype(F32)
             value = value * scale
-            direct_out[b] = value.astype(BF16)
+            direct_out[n] = value.astype(BF16)
             if b < 5:
-                turned_out[b] = value.T.astype(BF16)
+                turned_out[n] = value.T.astype(BF16)
         when_active(b, finish)
         send_direct(b, 0)
         if b < 5:
@@ -266,6 +287,19 @@
     direct_from = jnp.where(p == g, p, inner_of)
     has_turned = cross | ((p != g) & inner)
     turned_from = jnp.where(cross, far_in, inner_of)
+    middle_pair = cross & inner & ((g == 1) | (g == 2))
+    early_cell = middle_pair | (p == g)
+    mine_now = jnp.logical_not(early_cell) if late else early_cell
+    has_direct = has_direct & mine_now
+    has_turned = has_turned & mine_now
+    if late:
+        @pl.when(early_cell)
+        def _():
+            out_ref[...] = early_ref[...]
+    else:
+        @pl.when(jnp.logical_not(early_cell))
+        def _():
+            out_ref[...] = jnp.zeros_like(out_ref)
 
     @pl.when(has_direct)
     def _():
@@ -301,7 +335,7 @@
             def _():
                 out_ref[rr, ll] = turned[vv * 2 + cc].astype(F32)
 
-    for b in range(6):
+    for b in order:
         def sent(b=b):
             stage1(b).wait_send()
             for k in range(1, 4):
@@ -312,56 +346,60 @@
             send_turned(b, 1)
 
 
-def place(blocks, scale):
+def place(operands, scale, late):
+    n = 4 if late else 2
     return pl.pallas_call(
-        lambda *refs: place_kernel(scale, *refs),
+        lambda *refs: place_kernel(scale, late, *refs),
         out_shape=jax.ShapeDtypeStruct((512, 256), F32),
-        in_specs=[pl.BlockSpec(memory_space=pltpu.VMEM)] * 6,
+        in_specs=[pl.BlockSpec(memory_space=pltpu.VMEM)] * len(operands),
         out_specs=pl.BlockSpec(memory_space=pltpu.VMEM),
         scratch_shapes=[
-            pltpu.VMEM((6, 512, 256), BF16),
-            pltpu.VMEM((6, 512, 256), BF16),
-            pltpu.VMEM((6, 3, 128, 256), BF16),
-            pltpu.VMEM((6, 128, 256), BF16),
-            pltpu.VMEM((5, 256, 128), BF16),
+            pltpu.VMEM((n, 512, 256), BF16),
+            pltpu.VMEM((n, 512, 256), F32),
+            pltpu.VMEM((n, 512, 256), BF16),
+            pltpu.VMEM((n, 512, 256), BF16),
+            pltpu.VMEM((n, 3, 128, 256), BF16),
+            pltpu.VMEM((n, 128, 256), BF16),
+            pltpu.VMEM((n, 256, 128), BF16),
             pltpu.VMEM((512, 256), BF16),
             pltpu.VMEM((4, 256, 128), BF16),
-            pltpu.SemaphoreType.DMA((6,)),
-            pltpu.SemaphoreType.DMA((6,)),
-            pltpu.SemaphoreType.DMA((6, 3)),
-            pltpu.SemaphoreType.DMA((6, 3)),
-            pltpu.SemaphoreType.DMA((6,)),
-            pltpu.SemaphoreType.DMA((5,)),
+            pltpu.SemaphoreType.DMA((n,)),
+            pltpu.SemaphoreType.DMA((n,)),
+            pltpu.SemaphoreType.DMA((n, 3)),
+            pltpu.SemaphoreType.DMA((n, 3)),
+            pltpu.SemaphoreType.DMA((n,)),
+            pltpu.SemaphoreType.DMA((n,)),
             pltpu.SemaphoreType.DMA((4,)),
             pltpu.SemaphoreType.DMA((4,)),
         ],
         compiler_params=pltpu.CompilerParams(
-            collective_id=0, has_side_effects=True, vmem_limit_bytes=32 * 1024 * 1024
+            collective_id=int(late), has_side_effects=True, vmem_limit_bytes=40 * 1024 * 1024
         ),
-        name="place",
-    )(*blocks)
+        cost_estimate=pl.CostEstimate(flops=0, bytes_accessed=50_000_000, transcendentals=0),
+        name="place_late" if late else "place_early",
+    )(*operands)
 
 
 def gram_dot(a, b):
     return lax.dot_general(a, b, (((1,), (1,)), ((), ())), preferred_element_type=F32)
 
 
-def four_planes(away, keep, total_cells):
+def four_planes(field, away, keep, smoothed, total_cells):
     across = [(1, 2), (2, 1)]
     inward = [(0, 1), (3, 2)]
     far_in = lax.ppermute(away, "dp", across)
     near_away = lax.ppermute(away, "dp", inward)
     near_keep = lax.ppermute(keep, "dp", inward)
     far_out = lax.ppermute(near_away, "dp", across)
-    blocks = [
-        gram_dot(near_away, away) + gram_dot(near_keep, keep),
-        gram_dot(keep, far_in),
-        gram_dot(keep, far_out),
-        gram_dot(near_keep, far_in),
-        gram_dot(near_keep, far_out),
-        gram_dot(away, away) + gram_dot(keep, keep),
-    ]
-    return place([b.astype(BF16) for b in blocks], 1.0 / total_cells)
+    scale = 1.0 / total_cells
+    begun = gram_dot(near_away, away)
+    early = [gram_dot(keep, far_in).astype(BF16), gram_dot(field, field).astype(BF16)]
+    early = place(early, scale, False)
+    near_keep, far_out, far_in, begun, early, smoothed = lax.optimization_barrier(
+        (near_keep, far_out, far_in, begun, early, smoothed)
+    )
+    gram = place((near_keep, far_in, far_out, keep, begun, early), scale, True)
+    return smoothed, gram
 
 
 def ring(field, total_cells):
@@ -396,7 +434,9 @@
     middle, *halves = two_steps(flat, *first_halo(sensitivity), coeff, width, planes)
     (smoothed,) = two_steps(middle, *flat_halo(middle, width), coeff, width, False)
     if planes:
-        gram = four_planes(*halves, total_cells)
+        smoothed, gram = four_planes(
+            middle, *halves, smoothed.reshape(sensitivity.shape), total_cells
+        )
     else:
         gram = ring(middle, total_cells)
     return smoothed.reshape(sensitivity.shape), gram

time: 193 us -> 201 us (1.041)
  Pallas kernels: 69.1 us -> 95 us
  matrix products: 21.2 us -> 6.51 us
  waiting for transfers between devices: 47.4 us -> 44.4 us
    pallas_call x1 -> x2, Pallas kernels: 33.4 us -> 59.4 us  [place(): pl.pallas_call(lambda *refs: place_kernel(scale, late, *refs), out_shape=...]
    ppermute x1, waiting for transfers between devices: 15.4 us -> 0.01 us  [four_planes(): near_keep = lax.ppermute(keep, 'dp', inward)]
    dot_general x8 -> x3, matrix products: 21.2 us -> 6.51 us  [gram_dot(): lax.dot_general(a, b, (((1,), (1,)), ((), ())), preferred_element_type=F32)]
    ppermute x1, waiting for transfers between devices: 32 us -> 40.2 us  [four_planes(): near_away = lax.ppermute(away, 'dp', inward)]
    ppermute x2, waiting for transfers between devices: 0.01 us -> 2.39 us  [exchange(): low = lax.ppermute(tops, 'tile', forward)]
    unnamed x28 -> x24, local copies, waits for them, and re-layouts: 18.8 us -> 17.4 us
  transfers between devices with their start and end apart: 10 -> 10, of which waited for: 2 -> 3; matrix products, arithmetic and copies ran while one was open for 17% -> 14% of each run, Pallas kernels for 9% -> 18%
where the time goes in v3:
time: 201 us; the launch traced here: 199 us
  Pallas kernels  95 us (47%)
  waiting for transfers between devices  44.4 us (22%)
  starting transfers between devices  28.6 us (14%)
  local copies, waits for them, and re-layouts  23.1 us (11%)
  matrix products  6.51 us (3%)
    pallas_call x2, Pallas kernels, place(): pl.pallas_call(lambda *refs: place_kernel(scale, late, *refs), out_shape=...  59.4 us
    ppermute x1, waiting for transfers between devices, four_planes(): near_away = lax.ppermute(away, 'dp', inward)  40.2 us
    pallas_call x2, Pallas kernels, two_steps(): pl.pallas_call(lambda *refs: smooth_kernel(width, split, *refs), out_shap...  35.6 us
    unnamed x24, local copies, waits for them, and re-layouts  17.4 us
    ppermute x2, starting transfers between devices, exchange(): high = lax.ppermute(bottoms, 'tile', [(t, s) for s, t in forward])  7.47 us
    dot_general x3, matrix products, gram_dot(): lax.dot_general(a, b, (((1,), (1,)), ((), ())), preferred_element_type=F32)  6.51 us
    ppermute x1, starting transfers between devices, four_planes(): near_away = lax.ppermute(away, 'dp', inward)  4.8 us
    ppermute x1, starting transfers between devices, four_planes(): near_keep = lax.ppermute(keep, 'dp', inward)  4.06 us
  transfers between devices with their start and end apart: 10, of which 3 were waited for; matrix products, arithmetic and copies ran while one was open for 14% of the time, Pallas kernels for 18%

profile of v3, /device:TPU:6, one launch (start us, length us, event | category | flops | bytes accessed | tf_op | source)
XLA Modules:
  0.0 199.5 jit_solution(8341637282047041682)
XLA Ops:
  0.6 0.7 fusion.12
  1.4 1.9 collective-permute-start.2
  3.3 3.6 %collective-permute-start.3 = (f32[2,2,128]{2,1,0:T(2,128)S(1)}, f32[2,2,128]{2,1,0:T(2,128)S(1)}, u32[]{:S(2)}, u32[]{:S(2)}) collective-permute-start(f32[2,2,128]{2,1,0:T(2,128)S(1)} %get-tuple-element.34), channel_id=1, source_target_pairs={{1,0},{2,1},{3,2},{4,3},{5,4},{6,5},{7,6},{9,8},{10,9},{11,10},{12... | collective-permute-start | bytes 6152 | tf_op jit(solution)/shard_map/ppermute | solution.py:22
  6.9 3.0 %fusion.11 = (bf16[512,2,2,128]{3,2,1,0:T(2,128)(2,1)S(1)}, bf16[512,2,2,128]{3,2,1,0:T(2,128)(2,1)S(1)}) fusion(bf16[512,2,16,128]{3,2,1,0:T(8,128)(2,1)} %param.2), kind=kLoop, calls=%fused_computation.39 | loop fusion | bytes 2097152 | tf_op jit(solution)/shard_map/slice | solution.py:147
  10.0 0.7 copy.8
  10.7 0.2 copy.5
  10.9 1.9 collective-permute-start
  12.9 0.7 copy.9
  13.6 0.2 copy.7
  13.8 3.6 %collective-permute-start.1 = (bf16[512,512]{1,0:T(8,128)(2,1)S(1)}, bf16[512,512]{1,0:T(8,128)(2,1)S(1)}, u32[]{:S(2)}, u32[]{:S(2)}) collective-permute-start(bf16[512,512]{1,0:T(8,128)(2,1)S(1)} %copy.7), channel_id=1, source_target_pairs={{1,0},{2,1},{3,2},{4,3},{5,4},{6,5},{7,6},{9,8},{10,9},{11,10},{12... | collective-permute-start | bytes 1572872 | tf_op jit(solution)/shard_map/ppermute | solution.py:132
  17.6 8.4 %copy.13 = bf16[64,8,32,128]{3,1,2,0:T(8,128)(2,1)} copy(bf16[64,8,32,128]{3,2,1,0:T(8,128)(2,1)} %bitcast.18) | data formatting | bytes 8388608
  26.3 0.7 broadcast_select_fusion.refs_3_
  27.1 0.8 copy-done.2
  28.1 18.3 %two_steps.2 = (bf16[512,4096]{1,0:T(8,128)(2,1)}, bf16[512,2048]{1,0:T(8,128)(2,1)}, bf16[512,2048]{1,0:T(8,128)(2,1)}) custom-call(bf16[512,4096]{1,0:T(8,128)(2,1)} %bitcast.16, bf16[512,512]{1,0:T(8,128)(2,1)} %copy-done.2, bf16[512,512]{1,0:T(8,128)(2,1)} %copy-done.3, f32[6,36,128]{2,1,0:T(8,128)} %broadcast_select_fusion.refs_3_), custom_call_target="tpu_custom_call" | custom-call | flops 50331648 | bytes 16777216 | tf_op jit(solution)/shard_map/two_steps/pallas_call | solution.py:110
  46.3 4.8 %collective-permute-start.5 = (bf16[512,2048]{1,0:T(8,128)(2,1)}, bf16[512,2048]{1,0:T(8,128)(2,1)}, u32[]{:S(2)}, u32[]{:S(2)}) collective-permute-start(bf16[512,2048]{1,0:T(8,128)(2,1)} %get-tuple-element.12), channel_id=1, source_target_pairs={{0,8},{24,16},{1,9},{25,17},{2,10},{26,18},{3,11},{27,19},{4,12},{... | collective-permute-start | bytes 6291464 | tf_op jit(solution)/shard_map/ppermute | solution.py:391
  51.1 0.8 collective-permute-start.7
  51.9 4.1 %collective-permute-start.4 = (bf16[512,2048]{1,0:T(8,128)(2,1)}, bf16[512,2048]{1,0:T(8,128)(2,1)}, u32[]{:S(2)}, u32[]{:S(2)}) collective-permute-start(bf16[512,2048]{1,0:T(8,128)(2,1)} %get-tuple-element.11.refs_3_), channel_id=1, source_target_pairs={{0,8},{24,16},{1,9},{25,17},{2,10},{26,18},{3,11},{27,19},{4,12},{... | collective-permute-start | bytes 6291464 | tf_op jit(solution)/shard_map/ppermute | solution.py:392
  56.0 40.2 %collective-permute-done.5 = bf16[512,2048]{1,0:T(8,128)(2,1)} collective-permute-done((bf16[512,2048]{1,0:T(8,128)(2,1)}, bf16[512,2048]{1,0:T(8,128)(2,1)}, u32[]{:S(2)}, u32[]{:S(2)}) %collective-permute-start.5) | collective-permute-done | bytes 2097184 | tf_op jit(solution)/shard_map/ppermute | solution.py:391
  96.2 2.0 collective-permute-start.6
  98.2 1.4 fusion.10
  99.6 2.1 %collective-permute-start.8 = (bf16[512,512]{1,0:T(8,128)(2,1)S(1)}, bf16[512,512]{1,0:T(8,128)(2,1)S(1)}, u32[]{:S(2)}, u32[]{:S(2)}) collective-permute-start(bf16[512,512]{1,0:T(8,128)(2,1)S(1)} %pad_maximum_fusion), channel_id=1, source_target_pairs={{0,1},{1,2},{2,3},{3,4},{4,5},{5,6},{6,7},{8,9},{9,10},{10,11},{11... | collective-permute-start | bytes 1572872 | tf_op jit(solution)/shard_map/ppermute | solution.py:131
  101.7 3.8 %collective-permute-start.9 = (bf16[512,512]{1,0:T(8,128)(2,1)S(1)}, bf16[512,512]{1,0:T(8,128)(2,1)}, u32[]{:S(2)}, u32[]{:S(2)}) collective-permute-start(bf16[512,512]{1,0:T(8,128)(2,1)S(1)} %pad_maximum_fusion.1), channel_id=1, source_target_pairs={{1,0},{2,1},{3,2},{4,3},{5,4},{6,5},{7,6},{9,8},{10,9},{11,10},{12... | collective-permute-start | bytes 1572872 | tf_op jit(solution)/shard_map/ppermute | solution.py:132
  105.6 2.4 %convolution_convert_fusion.refs_1_ = bf16[512,512]{1,0:T(8,128)(2,1)S(1)} fusion(bf16[512,4096]{1,0:T(8,128)(2,1)S(1)} %copy-done.1), kind=kOutput, calls=%fused_computation.1 | convolution fusion | flops 2147745792 | bytes 4718592 | tf_op jit(solution)/shard_map/dot_general | solution.py:384
  107.9 2.4 %collective-permute-done.8.refs_1_ = bf16[512,512]{1,0:T(8,128)(2,1)S(1)} collective-permute-done((bf16[512,512]{1,0:T(8,128)(2,1)S(1)}, bf16[512,512]{1,0:T(8,128)(2,1)S(1)}, u32[]{:S(2)}, u32[]{:S(2)}) %collective-permute-start.8) | collective-permute-done | bytes 524320 | tf_op jit(solution)/shard_map/ppermute | solution.py:131
  110.3 1.7 collective-permute-done.9.refs_2_
  112.1 17.4 %two_steps.3 = bf16[512,4096]{1,0:T(8,128)(2,1)} custom-call(bf16[512,4096]{1,0:T(8,128)(2,1)} %get-tuple-element.13.refs_0_, bf16[512,512]{1,0:T(8,128)(2,1)} %copy-done.4, bf16[512,512]{1,0:T(8,128)(2,1)} %collective-permute-done.9.refs_2_, f32[6,36,128]{2,1,0:T(8,128)} %broadcast_select_fusion.refs_3_), custom_call_target="tpu_custom_call" | custom-call | flops 50331648 | bytes 16777216 | tf_op jit(solution)/shard_map/two_steps/pallas_call | solution.py:110
  129.4 5.6 %copy.11 = bf16[64,8,32,128]{3,2,1,0:T(8,128)(2,1)} copy(bf16[64,8,32,128]{3,1,2,0:T(8,128)(2,1)} %bitcast.17) | data formatting | bytes 8388608
  135.1 1.3 convolution_convert_fusion.1.refs_0_
  136.4 19.4 %place_early.1.refs_5_ = f32[512,256]{1,0:T(8,128)S(1)} custom-call(bf16[512,512]{1,0:T(8,128)(2,1)S(1)} %convolution_convert_fusion.1.refs_0_, bf16[512,512]{1,0:T(8,128)(2,1)S(1)} %convolution_convert_fusion.refs_1_), custom_call_target="tpu_custom_call" | custom-call | bytes 50000000 | tf_op jit(solution)/shard_map/place_early/pallas_call | solution.py:351
  155.7 2.9 %fusion.13.refs_4_ = f32[512,512]{1,0:T(8,128)S(1)} fusion(bf16[512,2048]{1,0:T(8,128)(2,1)} %collective-permute-done.5, bf16[512,2048]{1,0:T(8,128)(2,1)S(1)} %copy-done.6), kind=kOutput, calls=%fused_computation.41 | convolution fusion | flops 1073741824 | bytes 5242880 | tf_op jit(solution)/shard_map/dot_general | solution.py:384
  158.6 40.0 %place_late.1 = f32[512,256]{1,0:T(8,128)S(1)} custom-call(bf16[512,2048]{1,0:T(8,128)(2,1)} %collective-permute-done.4.refs_0_, bf16[512,2048]{1,0:T(8,128)(2,1)S(1)} %collective-permute-done.7.refs_1_, bf16[512,2048]{1,0:T(8,128)(2,1)} %collective-permute-done.6.refs_2_, bf16[512,2048]{1,0:T(8,128)(2,1)S(1)} %copy-done, f32[512,512]{1,0:T(8,128)S(1)} %fusion.13.refs_4_, ...), custom_call_target="tpu_custom_call" | custom-call | bytes 50000000 | tf_op jit(solution)/shard_map/place_late/pallas_call | solution.py:351
  198.7 0.8 copy.20
  (41 shorter events, 0.6 us)
Async XLA Ops:
  1.4 24.7 %collective-permute-start.2 = (f32[2,2,128]{2,1,0:T(2,128)S(1)}, f32[2,2,128]{2,1,0:T(2,128)S(1)}, u32[]{:S(2)}, u32[]{:S(2)}) collective-permute-start(f32[2,2,128]{2,1,0:T(2,128)S(1)} %get-tuple-element.33), channel_id=1, source_target_pairs={{0,1},{1,2},{2,3},{3,4},{4,5},{5,6},{6,7},{8,9},{9,10},{10,11},{11... | collective-permute-start | bytes 6152 | tf_op jit(solution)/shard_map/ppermute | solution.py:19
  3.3 22.8 %collective-permute-start.3 = (f32[2,2,128]{2,1,0:T(2,128)S(1)}, f32[2,2,128]{2,1,0:T(2,128)S(1)}, u32[]{:S(2)}, u32[]{:S(2)}) collective-permute-start(f32[2,2,128]{2,1,0:T(2,128)S(1)} %get-tuple-element.34), channel_id=1, source_target_pairs={{1,0},{2,1},{3,2},{4,3},{5,4},{6,5},{7,6},{9,8},{10,9},{11,10},{12... | collective-permute-start | bytes 6152 | tf_op jit(solution)/shard_map/ppermute | solution.py:22
  10.9 16.1 %collective-permute-start = (bf16[512,512]{1,0:T(8,128)(2,1)S(1)}, bf16[512,512]{1,0:T(8,128)(2,1)S(1)}, u32[]{:S(2)}, u32[]{:S(2)}) collective-permute-start(bf16[512,512]{1,0:T(8,128)(2,1)S(1)} %copy.5), channel_id=1, source_target_pairs={{0,1},{1,2},{2,3},{3,4},{4,5},{5,6},{6,7},{8,9},{9,10},{10,11},{11... | collective-permute-start | bytes 1572872 | tf_op jit(solution)/shard_map/ppermute | solution.py:131
  13.8 13.3 %collective-permute-start.1 = (bf16[512,512]{1,0:T(8,128)(2,1)S(1)}, bf16[512,512]{1,0:T(8,128)(2,1)S(1)}, u32[]{:S(2)}, u32[]{:S(2)}) collective-permute-start(bf16[512,512]{1,0:T(8,128)(2,1)S(1)} %copy.7), channel_id=1, source_target_pairs={{1,0},{2,1},{3,2},{4,3},{5,4},{6,5},{7,6},{9,8},{10,9},{11,10},{12... | collective-permute-start | bytes 1572872 | tf_op jit(solution)/shard_map/ppermute | solution.py:132
  17.6 8.5 %copy-start.5 = (f32[2,16,128]{2,1,0:T(8,128)S(1)}, f32[2,16,128]{2,1,0:T(8,128)}, u32[]{:S(2)}) copy-start(f32[2,16,128]{2,1,0:T(8,128)} %param.3) | copy-start | bytes 49156
  27.1 0.8 copy-start.2
  27.1 1.0 copy-start.3
  46.3 49.9 %collective-permute-start.5 = (bf16[512,2048]{1,0:T(8,128)(2,1)}, bf16[512,2048]{1,0:T(8,128)(2,1)}, u32[]{:S(2)}, u32[]{:S(2)}) collective-permute-start(bf16[512,2048]{1,0:T(8,128)(2,1)} %get-tuple-element.12), channel_id=1, source_target_pairs={{0,8},{24,16},{1,9},{25,17},{2,10},{26,18},{3,11},{27,19},{4,12},{... | collective-permute-start | bytes 6291464 | tf_op jit(solution)/shard_map/ppermute | solution.py:391
  51.1 83.9 %collective-permute-start.7 = (bf16[512,2048]{1,0:T(8,128)(2,1)}, bf16[512,2048]{1,0:T(8,128)(2,1)S(1)}, u32[]{:S(2)}, u32[]{:S(2)}) collective-permute-start(bf16[512,2048]{1,0:T(8,128)(2,1)} %get-tuple-element.12), channel_id=1, source_target_pairs={{8,16},{16,8},{9,17},{17,9},{10,18},{18,10},{11,19},{19,11},{12,20... | collective-permute-start | bytes 6291464 | tf_op jit(solution)/shard_map/ppermute | solution.py:390
  51.9 106.7 %collective-permute-start.4 = (bf16[512,2048]{1,0:T(8,128)(2,1)}, bf16[512,2048]{1,0:T(8,128)(2,1)}, u32[]{:S(2)}, u32[]{:S(2)}) collective-permute-start(bf16[512,2048]{1,0:T(8,128)(2,1)} %get-tuple-element.11.refs_3_), channel_id=1, source_target_pairs={{0,8},{24,16},{1,9},{25,17},{2,10},{26,18},{3,11},{27,19},{4,12},{... | collective-permute-start | bytes 6291464 | tf_op jit(solution)/shard_map/ppermute | solution.py:392
  96.2 62.4 %collective-permute-start.6 = (bf16[512,2048]{1,0:T(8,128)(2,1)}, bf16[512,2048]{1,0:T(8,128)(2,1)}, u32[]{:S(2)}, u32[]{:S(2)}) collective-permute-start(bf16[512,2048]{1,0:T(8,128)(2,1)} %collective-permute-done.5), channel_id=1, source_target_pairs={{8,16},{16,8},{9,17},{17,9},{10,18},{18,10},{11,19},{19,11},{12,20... | collective-permute-start | bytes 6291464 | tf_op jit(solution)/shard_map/ppermute | solution.py:393
  98.2 7.4 %copy-start.1 = (bf16[512,4096]{1,0:T(8,128)(2,1)S(1)}, bf16[512,4096]{1,0:T(8,128)(2,1)}, u32[]{:S(2)}) copy-start(bf16[512,4096]{1,0:T(8,128)(2,1)} %get-tuple-element.13.refs_0_) | copy-start | bytes 12582916
  99.6 10.7 %collective-permute-start.8 = (bf16[512,512]{1,0:T(8,128)(2,1)S(1)}, bf16[512,512]{1,0:T(8,128)(2,1)S(1)}, u32[]{:S(2)}, u32[]{:S(2)}) collective-permute-start(bf16[512,512]{1,0:T(8,128)(2,1)S(1)} %pad_maximum_fusion), channel_id=1, source_target_pairs={{0,1},{1,2},{2,3},{3,4},{4,5},{5,6},{6,7},{8,9},{9,10},{10,11},{11... | collective-permute-start | bytes 1572872 | tf_op jit(solution)/shard_map/ppermute | solution.py:131
  101.7 10.3 %collective-permute-start.9 = (bf16[512,512]{1,0:T(8,128)(2,1)S(1)}, bf16[512,512]{1,0:T(8,128)(2,1)}, u32[]{:S(2)}, u32[]{:S(2)}) collective-permute-start(bf16[512,512]{1,0:T(8,128)(2,1)S(1)} %pad_maximum_fusion.1), channel_id=1, source_target_pairs={{1,0},{2,1},{3,2},{4,3},{5,4},{6,5},{7,6},{9,8},{10,9},{11,10},{12... | collective-permute-start | bytes 1572872 | tf_op jit(solution)/shard_map/ppermute | solution.py:132
  110.3 1.7 copy-start.4
  129.4 5.6 %copy-start = (bf16[512,2048]{1,0:T(8,128)(2,1)S(1)}, bf16[512,2048]{1,0:T(8,128)(2,1)}, u32[]{:S(2)}) copy-start(bf16[512,2048]{1,0:T(8,128)(2,1)} %get-tuple-element.11.refs_3_) | copy-start | bytes 6291460
  135.1 20.7 %copy-start.6 = (bf16[512,2048]{1,0:T(8,128)(2,1)S(1)}, bf16[512,2048]{1,0:T(8,128)(2,1)}, u32[]{:S(2)}) copy-start(bf16[512,2048]{1,0:T(8,128)(2,1)} %get-tuple-element.12) | copy-start | bytes 6291460

commit v4 on v3

--- a/solution.py
+++ b/solution.py
@@ -390,6 +390,7 @@
     far_in = lax.ppermute(away, "dp", across)
     near_away = lax.ppermute(away, "dp", inward)
     near_keep = lax.ppermute(keep, "dp", inward)
+    near_away, smoothed = lax.optimization_barrier((near_away, smoothed))
     far_out = lax.ppermute(near_away, "dp", across)
     scale = 1.0 / total_cells
     begun = gram_dot(near_away, away)

time: 201 us -> 187 us (0.930)
  waiting for transfers between devices: 44.4 us -> 26.6 us
  Pallas kernels: 95 us -> 97.8 us
    ppermute x1, waiting for transfers between devices: 40.2 us -> 5.51 us  [four_planes(): near_away = lax.ppermute(away, 'dp', inward)]
    ppermute x1, waiting for transfers between devices: 0.01 us -> 17.3 us  [four_planes(): near_keep = lax.ppermute(keep, 'dp', inward)]
    pallas_call x2, Pallas kernels: 59.4 us -> 62.1 us  [place(): pl.pallas_call(lambda *refs: place_kernel(scale, late, *refs), out_shape=...]
    unnamed x24 -> x26, local copies, waits for them, and re-layouts: 17.4 us -> 18.1 us
  transfers between devices with their start and end apart: 10 -> 10, of which waited for: 3 -> 4; matrix products, arithmetic and copies ran while one was open for 14% -> 16% of each run, Pallas kernels for 18% -> 18%
where the time goes in v4:
time: 187 us; the launch traced here: 186 us
  Pallas kernels  97.8 us (52%)
  starting transfers between devices  27.3 us (15%)
  waiting for transfers between devices  26.6 us (14%)
  local copies, waits for them, and re-layouts  23.9 us (13%)
  matrix products  8.25 us (4%)
    pallas_call x2, Pallas kernels, place(): pl.pallas_call(lambda *refs: place_kernel(scale, late, *refs), out_shape=...  62.1 us
    pallas_call x2, Pallas kernels, two_steps(): pl.pallas_call(lambda *refs: smooth_kernel(width, split, *refs), out_shap...  35.7 us
    unnamed x26, local copies, waits for them, and re-layouts  18.1 us
    ppermute x1, waiting for transfers between devices, four_planes(): near_keep = lax.ppermute(keep, 'dp', inward)  17.3 us
    dot_general x3, matrix products, gram_dot(): lax.dot_general(a, b, (((1,), (1,)), ((), ())), preferred_element_type=F32)  8.25 us
    ppermute x2, starting transfers between devices, exchange(): high = lax.ppermute(bottoms, 'tile', [(t, s) for s, t in forward])  7.28 us
    ppermute x1, waiting for transfers between devices, four_planes(): near_away = lax.ppermute(away, 'dp', inward)  5.51 us
    ppermute x1, starting transfers between devices, four_planes(): near_away = lax.ppermute(away, 'dp', inward)  4.79 us
  transfers between devices with their start and end apart: 10, of which 4 were waited for; matrix products, arithmetic and copies ran while one was open for 16% of the time, Pallas kernels for 18%

profile of v4, /device:TPU:6, one launch (start us, length us, event | category | flops | bytes accessed | tf_op | source)
XLA Modules:
  0.0 185.8 jit_solution(8372652346290530870)
XLA Ops:
  0.6 0.7 fusion.12
  1.4 1.9 %collective-permute-start.2 = (f32[2,2,128]{2,1,0:T(2,128)S(1)}, f32[2,2,128]{2,1,0:T(2,128)S(1)}, u32[]{:S(2)}, u32[]{:S(2)}) collective-permute-start(f32[2,2,128]{2,1,0:T(2,128)S(1)} %get-tuple-element.37), channel_id=1, source_target_pairs={{0,1},{1,2},{2,3},{3,4},{4,5},{5,6},{6,7},{8,9},{9,10},{10,11},{11... | collective-permute-start | bytes 6152 | tf_op jit(solution)/shard_map/ppermute | solution.py:19
  3.3 3.6 %collective-permute-start.3 = (f32[2,2,128]{2,1,0:T(2,128)S(1)}, f32[2,2,128]{2,1,0:T(2,128)S(1)}, u32[]{:S(2)}, u32[]{:S(2)}) collective-permute-start(f32[2,2,128]{2,1,0:T(2,128)S(1)} %get-tuple-element.38), channel_id=1, source_target_pairs={{1,0},{2,1},{3,2},{4,3},{5,4},{6,5},{7,6},{9,8},{10,9},{11,10},{12... | collective-permute-start | bytes 6152 | tf_op jit(solution)/shard_map/ppermute | solution.py:22
  6.9 3.0 %fusion.11 = (bf16[512,2,2,128]{3,2,1,0:T(2,128)(2,1)S(1)}, bf16[512,2,2,128]{3,2,1,0:T(2,128)(2,1)S(1)}) fusion(bf16[512,2,16,128]{3,2,1,0:T(8,128)(2,1)} %param.2), kind=kLoop, calls=%fused_computation.39 | loop fusion | bytes 2097152 | tf_op jit(solution)/shard_map/slice | solution.py:147
  10.0 0.7 copy.8
  10.9 1.9 %collective-permute-start = (bf16[512,512]{1,0:T(8,128)(2,1)S(1)}, bf16[512,512]{1,0:T(8,128)(2,1)S(1)}, u32[]{:S(2)}, u32[]{:S(2)}) collective-permute-start(bf16[512,512]{1,0:T(8,128)(2,1)S(1)} %copy.5), channel_id=1, source_target_pairs={{0,1},{1,2},{2,3},{3,4},{4,5},{5,6},{6,7},{8,9},{9,10},{10,11},{11... | collective-permute-start | bytes 1572872 | tf_op jit(solution)/shard_map/ppermute | solution.py:131
  12.9 0.7 copy.9
  13.8 3.6 %collective-permute-start.1 = (bf16[512,512]{1,0:T(8,128)(2,1)S(1)}, bf16[512,512]{1,0:T(8,128)(2,1)S(1)}, u32[]{:S(2)}, u32[]{:S(2)}) collective-permute-start(bf16[512,512]{1,0:T(8,128)(2,1)S(1)} %copy.7), channel_id=1, source_target_pairs={{1,0},{2,1},{3,2},{4,3},{5,4},{6,5},{7,6},{9,8},{10,9},{11,10},{12... | collective-permute-start | bytes 1572872 | tf_op jit(solution)/shard_map/ppermute | solution.py:132
  17.6 8.4 %copy.13 = bf16[64,8,32,128]{3,1,2,0:T(8,128)(2,1)} copy(bf16[64,8,32,128]{3,2,1,0:T(8,128)(2,1)} %bitcast.18) | data formatting | bytes 8388608
  26.3 0.7 broadcast_select_fusion.refs_3_
  27.1 0.8 copy-done.2
  28.1 18.3 %two_steps.2 = (bf16[512,4096]{1,0:T(8,128)(2,1)}, bf16[512,2048]{1,0:T(8,128)(2,1)}, bf16[512,2048]{1,0:T(8,128)(2,1)}) custom-call(bf16[512,4096]{1,0:T(8,128)(2,1)} %bitcast.16, bf16[512,512]{1,0:T(8,128)(2,1)} %copy-done.2, bf16[512,512]{1,0:T(8,128)(2,1)} %copy-done.3, f32[6,36,128]{2,1,0:T(8,128)} %broadcast_select_fusion.refs_3_), custom_call_target="tpu_custom_call" | custom-call | flops 50331648 | bytes 16777216 | tf_op jit(solution)/shard_map/two_steps/pallas_call | solution.py:110
  46.4 4.8 %collective-permute-start.5 = (bf16[512,2048]{1,0:T(8,128)(2,1)}, bf16[512,2048]{1,0:T(8,128)(2,1)}, u32[]{:S(2)}, u32[]{:S(2)}) collective-permute-start(bf16[512,2048]{1,0:T(8,128)(2,1)} %get-tuple-element.14), channel_id=1, source_target_pairs={{0,8},{24,16},{1,9},{25,17},{2,10},{26,18},{3,11},{27,19},{4,12},{... | collective-permute-start | bytes 6291464 | tf_op jit(solution)/shard_map/ppermute | solution.py:391
  51.2 2.0 %collective-permute-start.9 = (bf16[512,2048]{1,0:T(8,128)(2,1)}, bf16[512,2048]{1,0:T(8,128)(2,1)}, u32[]{:S(2)}, u32[]{:S(2)}) collective-permute-start(bf16[512,2048]{1,0:T(8,128)(2,1)} %get-tuple-element.14), channel_id=1, source_target_pairs={{8,16},{16,8},{9,17},{17,9},{10,18},{18,10},{11,19},{19,11},{12,20... | collective-permute-start | bytes 6291464 | tf_op jit(solution)/shard_map/ppermute | solution.py:390
  53.2 1.4 fusion.10
  54.6 1.9 %collective-permute-start.6 = (bf16[512,512]{1,0:T(8,128)(2,1)S(1)}, bf16[512,512]{1,0:T(8,128)(2,1)S(1)}, u32[]{:S(2)}, u32[]{:S(2)}) collective-permute-start(bf16[512,512]{1,0:T(8,128)(2,1)S(1)} %pad_maximum_fusion), channel_id=1, source_target_pairs={{0,1},{1,2},{2,3},{3,4},{4,5},{5,6},{6,7},{8,9},{9,10},{10,11},{11... | collective-permute-start | bytes 1572872 | tf_op jit(solution)/shard_map/ppermute | solution.py:131
  56.6 3.6 %collective-permute-start.7 = (bf16[512,512]{1,0:T(8,128)(2,1)S(1)}, bf16[512,512]{1,0:T(8,128)(2,1)S(1)}, u32[]{:S(2)}, u32[]{:S(2)}) collective-permute-start(bf16[512,512]{1,0:T(8,128)(2,1)S(1)} %pad_maximum_fusion.1), channel_id=1, source_target_pairs={{1,0},{2,1},{3,2},{4,3},{5,4},{6,5},{7,6},{9,8},{10,9},{11,10},{12... | collective-permute-start | bytes 1572872 | tf_op jit(solution)/shard_map/ppermute | solution.py:132
  60.3 2.8 %collective-permute-start.4 = (bf16[512,2048]{1,0:T(8,128)(2,1)S(1)}, bf16[512,2048]{1,0:T(8,128)(2,1)}, u32[]{:S(2)}, u32[]{:S(2)}) collective-permute-start(bf16[512,2048]{1,0:T(8,128)(2,1)S(1)} %copy-done), channel_id=1, source_target_pairs={{0,8},{24,16},{1,9},{25,17},{2,10},{26,18},{3,11},{27,19},{4,12},{... | collective-permute-start | bytes 6291464 | tf_op jit(solution)/shard_map/ppermute | solution.py:392
  63.1 2.1 %collective-permute-done.6.refs_1_ = bf16[512,512]{1,0:T(8,128)(2,1)S(1)} collective-permute-done((bf16[512,512]{1,0:T(8,128)(2,1)S(1)}, bf16[512,512]{1,0:T(8,128)(2,1)S(1)}, u32[]{:S(2)}, u32[]{:S(2)}) %collective-permute-start.6) | collective-permute-done | bytes 524320 | tf_op jit(solution)/shard_map/ppermute | solution.py:131
  65.2 1.7 collective-permute-done.7.refs_2_
  66.9 0.8 copy-done.5
  67.7 17.4 %two_steps.3 = bf16[512,4096]{1,0:T(8,128)(2,1)} custom-call(bf16[512,4096]{1,0:T(8,128)(2,1)} %get-tuple-element.15.refs_0_, bf16[512,512]{1,0:T(8,128)(2,1)} %copy-done.4, bf16[512,512]{1,0:T(8,128)(2,1)} %copy-done.5, f32[6,36,128]{2,1,0:T(8,128)} %broadcast_select_fusion.refs_3_), custom_call_target="tpu_custom_call" | custom-call | flops 50331648 | bytes 16777216 | tf_op jit(solution)/shard_map/two_steps/pallas_call | solution.py:110
  85.1 5.6 %copy.11 = bf16[64,8,32,128]{3,2,1,0:T(8,128)(2,1)} copy(bf16[64,8,32,128]{3,1,2,0:T(8,128)(2,1)} %bitcast.17) | data formatting | bytes 8388608
  90.7 5.5 %collective-permute-done.5 = bf16[512,2048]{1,0:T(8,128)(2,1)} collective-permute-done((bf16[512,2048]{1,0:T(8,128)(2,1)}, bf16[512,2048]{1,0:T(8,128)(2,1)}, u32[]{:S(2)}, u32[]{:S(2)}) %collective-permute-start.5) | collective-permute-done | bytes 2097184 | tf_op jit(solution)/shard_map/ppermute | solution.py:391
  96.2 1.0 collective-permute-start.8
  97.2 2.4 %convolution_convert_fusion.refs_1_ = bf16[512,512]{1,0:T(8,128)(2,1)S(1)} fusion(bf16[512,4096]{1,0:T(8,128)(2,1)S(1)} %copy-done.1), kind=kOutput, calls=%fused_computation.1 | convolution fusion | flops 2147745792 | bytes 4718592 | tf_op jit(solution)/shard_map/dot_general | solution.py:384
  99.6 3.0 %convolution_convert_fusion.1.refs_0_ = bf16[512,512]{1,0:T(8,128)(2,1)S(1)} fusion(bf16[512,2048]{1,0:T(8,128)(2,1)S(1)} %copy-done, bf16[512,2048]{1,0:T(8,128)(2,1)} %collective-permute-done.9.refs_1_), kind=kOutput, calls=%fused_computation.2 | convolution fusion | flops 1074003968 | bytes 4718592 | tf_op jit(solution)/shard_map/dot_general | solution.py:384
  102.6 15.9 %place_early.1.refs_5_ = f32[512,256]{1,0:T(8,128)S(1)} custom-call(bf16[512,512]{1,0:T(8,128)(2,1)S(1)} %convolution_convert_fusion.1.refs_0_, bf16[512,512]{1,0:T(8,128)(2,1)S(1)} %convolution_convert_fusion.refs_1_), custom_call_target="tpu_custom_call" | custom-call | bytes 50000000 | tf_op jit(solution)/shard_map/place_early/pallas_call | solution.py:351
  118.6 2.9 %fusion.13.refs_4_ = f32[512,512]{1,0:T(8,128)S(1)} fusion(bf16[512,2048]{1,0:T(8,128)(2,1)} %collective-permute-done.5, bf16[512,2048]{1,0:T(8,128)(2,1)S(1)} %copy-done.7), kind=kOutput, calls=%fused_computation.41 | convolution fusion | flops 1073741824 | bytes 5242880 | tf_op jit(solution)/shard_map/dot_general | solution.py:384
  121.5 17.3 %collective-permute-done.4.refs_0_ = bf16[512,2048]{1,0:T(8,128)(2,1)} collective-permute-done((bf16[512,2048]{1,0:T(8,128)(2,1)S(1)}, bf16[512,2048]{1,0:T(8,128)(2,1)}, u32[]{:S(2)}, u32[]{:S(2)}) %collective-permute-start.4) | collective-permute-done | bytes 2097184 | tf_op jit(solution)/shard_map/ppermute | solution.py:392
  138.8 46.2 %place_late.1 = f32[512,256]{1,0:T(8,128)S(1)} custom-call(bf16[512,2048]{1,0:T(8,128)(2,1)} %collective-permute-done.4.refs_0_, bf16[512,2048]{1,0:T(8,128)(2,1)} %collective-permute-done.9.refs_1_, bf16[512,2048]{1,0:T(8,128)(2,1)S(1)} %collective-permute-done.8.refs_2_, bf16[512,2048]{1,0:T(8,128)(2,1)S(1)} %copy-done, f32[512,512]{1,0:T(8,128)S(1)} %fusion.13.refs_4_, ...), custom_call_target="tpu_custom_call" | custom-call | bytes 50000000 | tf_op jit(solution)/shard_map/place_late/pallas_call | solution.py:351
  185.0 0.8 copy.20
  (43 shorter events, 1.0 us)
Async XLA Ops:
  1.4 24.7 %collective-permute-start.2 = (f32[2,2,128]{2,1,0:T(2,128)S(1)}, f32[2,2,128]{2,1,0:T(2,128)S(1)}, u32[]{:S(2)}, u32[]{:S(2)}) collective-permute-start(f32[2,2,128]{2,1,0:T(2,128)S(1)} %get-tuple-element.37), channel_id=1, source_target_pairs={{0,1},{1,2},{2,3},{3,4},{4,5},{5,6},{6,7},{8,9},{9,10},{10,11},{11... | collective-permute-start | bytes 6152 | tf_op jit(solution)/shard_map/ppermute | solution.py:19
  3.3 22.8 %collective-permute-start.3 = (f32[2,2,128]{2,1,0:T(2,128)S(1)}, f32[2,2,128]{2,1,0:T(2,128)S(1)}, u32[]{:S(2)}, u32[]{:S(2)}) collective-permute-start(f32[2,2,128]{2,1,0:T(2,128)S(1)} %get-tuple-element.38), channel_id=1, source_target_pairs={{1,0},{2,1},{3,2},{4,3},{5,4},{6,5},{7,6},{9,8},{10,9},{11,10},{12... | collective-permute-start | bytes 6152 | tf_op jit(solution)/shard_map/ppermute | solution.py:22
  10.9 16.1 %collective-permute-start = (bf16[512,512]{1,0:T(8,128)(2,1)S(1)}, bf16[512,512]{1,0:T(8,128)(2,1)S(1)}, u32[]{:S(2)}, u32[]{:S(2)}) collective-permute-start(bf16[512,512]{1,0:T(8,128)(2,1)S(1)} %copy.5), channel_id=1, source_target_pairs={{0,1},{1,2},{2,3},{3,4},{4,5},{5,6},{6,7},{8,9},{9,10},{10,11},{11... | collective-permute-start | bytes 1572872 | tf_op jit(solution)/shard_map/ppermute | solution.py:131
  13.8 13.3 %collective-permute-start.1 = (bf16[512,512]{1,0:T(8,128)(2,1)S(1)}, bf16[512,512]{1,0:T(8,128)(2,1)S(1)}, u32[]{:S(2)}, u32[]{:S(2)}) collective-permute-start(bf16[512,512]{1,0:T(8,128)(2,1)S(1)} %copy.7), channel_id=1, source_target_pairs={{1,0},{2,1},{3,2},{4,3},{5,4},{6,5},{7,6},{9,8},{10,9},{11,10},{12... | collective-permute-start | bytes 1572872 | tf_op jit(solution)/shard_map/ppermute | solution.py:132
  17.6 8.5 %copy-start.6 = (f32[2,16,128]{2,1,0:T(8,128)S(1)}, f32[2,16,128]{2,1,0:T(8,128)}, u32[]{:S(2)}) copy-start(f32[2,16,128]{2,1,0:T(8,128)} %param.3) | copy-start | bytes 49156
  27.1 0.8 copy-start.2
  27.1 1.0 copy-start.3
  46.4 49.9 %collective-permute-start.5 = (bf16[512,2048]{1,0:T(8,128)(2,1)}, bf16[512,2048]{1,0:T(8,128)(2,1)}, u32[]{:S(2)}, u32[]{:S(2)}) collective-permute-start(bf16[512,2048]{1,0:T(8,128)(2,1)} %get-tuple-element.14), channel_id=1, source_target_pairs={{0,8},{24,16},{1,9},{25,17},{2,10},{26,18},{3,11},{27,19},{4,12},{... | collective-permute-start | bytes 6291464 | tf_op jit(solution)/shard_map/ppermute | solution.py:391
  51.2 48.4 %collective-permute-start.9 = (bf16[512,2048]{1,0:T(8,128)(2,1)}, bf16[512,2048]{1,0:T(8,128)(2,1)}, u32[]{:S(2)}, u32[]{:S(2)}) collective-permute-start(bf16[512,2048]{1,0:T(8,128)(2,1)} %get-tuple-element.14), channel_id=1, source_target_pairs={{8,16},{16,8},{9,17},{17,9},{10,18},{18,10},{11,19},{19,11},{12,20... | collective-permute-start | bytes 6291464 | tf_op jit(solution)/shard_map/ppermute | solution.py:390
  53.2 7.1 %copy-start = (bf16[512,2048]{1,0:T(8,128)(2,1)S(1)}, bf16[512,2048]{1,0:T(8,128)(2,1)}, u32[]{:S(2)}) copy-start(bf16[512,2048]{1,0:T(8,128)(2,1)} %get-tuple-element.13.refs_3_) | copy-start | bytes 6291460
  54.6 10.6 %collective-permute-start.6 = (bf16[512,512]{1,0:T(8,128)(2,1)S(1)}, bf16[512,512]{1,0:T(8,128)(2,1)S(1)}, u32[]{:S(2)}, u32[]{:S(2)}) collective-permute-start(bf16[512,512]{1,0:T(8,128)(2,1)S(1)} %pad_maximum_fusion), channel_id=1, source_target_pairs={{0,1},{1,2},{2,3},{3,4},{4,5},{5,6},{6,7},{8,9},{9,10},{10,11},{11... | collective-permute-start | bytes 1572872 | tf_op jit(solution)/shard_map/ppermute | solution.py:131
  56.6 10.3 %collective-permute-start.7 = (bf16[512,512]{1,0:T(8,128)(2,1)S(1)}, bf16[512,512]{1,0:T(8,128)(2,1)S(1)}, u32[]{:S(2)}, u32[]{:S(2)}) collective-permute-start(bf16[512,512]{1,0:T(8,128)(2,1)S(1)} %pad_maximum_fusion.1), channel_id=1, source_target_pairs={{1,0},{2,1},{3,2},{4,3},{5,4},{6,5},{7,6},{9,8},{10,9},{11,10},{12... | collective-permute-start | bytes 1572872 | tf_op jit(solution)/shard_map/ppermute | solution.py:132
  60.3 78.5 %collective-permute-start.4 = (bf16[512,2048]{1,0:T(8,128)(2,1)S(1)}, bf16[512,2048]{1,0:T(8,128)(2,1)}, u32[]{:S(2)}, u32[]{:S(2)}) collective-permute-start(bf16[512,2048]{1,0:T(8,128)(2,1)S(1)} %copy-done), channel_id=1, source_target_pairs={{0,8},{24,16},{1,9},{25,17},{2,10},{26,18},{3,11},{27,19},{4,12},{... | collective-permute-start | bytes 6291464 | tf_op jit(solution)/shard_map/ppermute | solution.py:392
  65.2 1.7 copy-start.4
  66.9 0.8 copy-start.5
  85.1 12.1 %copy-start.1 = (bf16[512,4096]{1,0:T(8,128)(2,1)S(1)}, bf16[512,4096]{1,0:T(8,128)(2,1)}, u32[]{:S(2)}) copy-start(bf16[512,4096]{1,0:T(8,128)(2,1)} %get-tuple-element.15.refs_0_) | copy-start | bytes 12582916
  96.2 42.6 %collective-permute-start.8 = (bf16[512,2048]{1,0:T(8,128)(2,1)}, bf16[512,2048]{1,0:T(8,128)(2,1)S(1)}, u32[]{:S(2)}, u32[]{:S(2)}) collective-permute-start(bf16[512,2048]{1,0:T(8,128)(2,1)} %collective-permute-done.5), channel_id=1, source_target_pairs={{8,16},{16,8},{9,17},{17,9},{10,18},{18,10},{11,19},{19,11},{12,20... | collective-permute-start | bytes 6291464 | tf_op jit(solution)/shard_map/ppermute | solution.py:394
  99.6 19.0 %copy-start.7 = (bf16[512,2048]{1,0:T(8,128)(2,1)S(1)}, bf16[512,2048]{1,0:T(8,128)(2,1)}, u32[]{:S(2)}) copy-start(bf16[512,2048]{1,0:T(8,128)(2,1)} %get-tuple-element.14) | copy-start | bytes 6291460

commit v5 on v4

--- a/solution.py
+++ b/solution.py
@@ -149,19 +149,19 @@
 
 
 def place_kernel(scale, late, *refs):
-    order = (3, 0, 2, 4) if late else (1, 5)
+    order = (1, 3, 0, 2, 4) if late else (5,)
     slot_of = {b: n for n, b in enumerate(order)}
     if late:
-        near_ref, far_in_ref, far_out_ref, keep_ref, begun_ref, early_ref = refs[:6]
-        refs = refs[6:]
+        near_ref, far_in_ref, far_out_ref, keep_ref, begun_ref, ready_ref, early_ref = refs[:7]
+        refs = refs[7:]
     else:
-        block_refs, refs = refs[:2], refs[2:]
+        ready_ref, refs = refs[0], refs[1:]
     (out_ref, outgoing, own, partner, half_out, quarter, direct_out, turned_out, direct, turned,
      s1_send, s1_recv, s2_send, s2_recv, d_send, t_send, d_recv, t_recv) = refs
 
     def product(b, cols):
-        if not late:
-            return block_refs[slot_of[b]][:, cols].astype(F32)
+        if b in (1, 5):
+            return ready_ref[:, cols].astype(F32)
         rows_ref = keep_ref if b == 2 else near_ref
         cols_ref = {0: keep_ref, 2: far_out_ref, 3: far_in_ref, 4: far_out_ref}[b]
         value = gram_dot(rows_ref[...], cols_ref[cols, :])
@@ -287,8 +287,7 @@
     direct_from = jnp.where(p == g, p, inner_of)
     has_turned = cross | ((p != g) & inner)
     turned_from = jnp.where(cross, far_in, inner_of)
-    middle_pair = cross & inner & ((g == 1) | (g == 2))
-    early_cell = middle_pair | (p == g)
+    early_cell = p == g
     mine_now = jnp.logical_not(early_cell) if late else early_cell
     has_direct = has_direct & mine_now
     has_turned = has_turned & mine_now
@@ -347,7 +346,7 @@
 
 
 def place(operands, scale, late):
-    n = 4 if late else 2
+    n = 5 if late else 1
     return pl.pallas_call(
         lambda *refs: place_kernel(scale, late, *refs),
         out_shape=jax.ShapeDtypeStruct((512, 256), F32),
@@ -394,12 +393,12 @@
     far_out = lax.ppermute(near_away, "dp", across)
     scale = 1.0 / total_cells
     begun = gram_dot(near_away, away)
-    early = [gram_dot(keep, far_in).astype(BF16), gram_dot(field, field).astype(BF16)]
-    early = place(early, scale, False)
-    near_keep, far_out, far_in, begun, early, smoothed = lax.optimization_barrier(
-        (near_keep, far_out, far_in, begun, early, smoothed)
+    ready = gram_dot(keep, far_in).astype(BF16)
+    early = place([gram_dot(field, field).astype(BF16)], scale, False)
+    near_keep, far_out, far_in, begun, ready, early, smoothed = lax.optimization_barrier(
+        (near_keep, far_out, far_in, begun, ready, early, smoothed)
     )
-    gram = place((near_keep, far_in, far_out, keep, begun, early), scale, True)
+    gram = place((near_keep, far_in, far_out, keep, begun, ready, early), scale, True)
     return smoothed, gram
 
 

time: 187 us -> 188 us (level)
    ppermute x2, waiting for transfers between devices: 2.08 us -> 0.07 us  [exchange(): low = lax.ppermute(tops, 'tile', forward)]
    ppermute x1, waiting for transfers between devices: 5.51 us -> 7.51 us  [four_planes(): near_away = lax.ppermute(away, 'dp', inward)]
    unnamed x26 -> x24, local copies, waits for them, and re-layouts: 18.1 us -> 18.1 us
where the time goes in v5:
time: 188 us; the launch traced here: 187 us
  Pallas kernels  98.8 us (53%)
  starting transfers between devices  27.3 us (15%)
  waiting for transfers between devices  26.3 us (14%)
  local copies, waits for them, and re-layouts  23.9 us (13%)
  matrix products  8.73 us (5%)
    pallas_call x2, Pallas kernels, place(): pl.pallas_call(lambda *refs: place_kernel(scale, late, *refs), out_shape=...  63.1 us
    pallas_call x2, Pallas kernels, two_steps(): pl.pallas_call(lambda *refs: smooth_kernel(width, split, *refs), out_shap...  35.7 us
    unnamed x24, local copies, waits for them, and re-layouts  18.1 us
    ppermute x1, waiting for transfers between devices, four_planes(): near_keep = lax.ppermute(keep, 'dp', inward)  16.9 us
    dot_general x3, matrix products, gram_dot(): lax.dot_general(a, b, (((1,), (1,)), ((), ())), preferred_element_type=F32)  8.73 us
    ppermute x1, waiting for transfers between devices, four_planes(): near_away = lax.ppermute(away, 'dp', inward)  7.51 us
    ppermute x2, starting transfers between devices, exchange(): high = lax.ppermute(bottoms, 'tile', [(t, s) for s, t in forward])  7.28 us
    ppermute x1, starting transfers between devices, four_planes(): near_away = lax.ppermute(away, 'dp', inward)  4.8 us
  transfers between devices with their start and end apart: 10, of which 4 were waited for; matrix products, arithmetic and copies ran while one was open for 16% of the time, Pallas kernels for 18%

profile of v5, /device:TPU:6, one launch (start us, length us, event | category | flops | bytes accessed | tf_op | source)
XLA Modules:
  0.0 186.9 jit_solution(9736546594831386052)
XLA Ops:
  0.6 0.7 fusion.12
  1.4 1.9 %collective-permute-start.2 = (f32[2,2,128]{2,1,0:T(2,128)S(1)}, f32[2,2,128]{2,1,0:T(2,128)S(1)}, u32[]{:S(2)}, u32[]{:S(2)}) collective-permute-start(f32[2,2,128]{2,1,0:T(2,128)S(1)} %get-tuple-element.39), channel_id=1, source_target_pairs={{0,1},{1,2},{2,3},{3,4},{4,5},{5,6},{6,7},{8,9},{9,10},{10,11},{11... | collective-permute-start | bytes 6152 | tf_op jit(solution)/shard_map/ppermute | solution.py:19
  3.3 3.6 %collective-permute-start.3 = (f32[2,2,128]{2,1,0:T(2,128)S(1)}, f32[2,2,128]{2,1,0:T(2,128)S(1)}, u32[]{:S(2)}, u32[]{:S(2)}) collective-permute-start(f32[2,2,128]{2,1,0:T(2,128)S(1)} %get-tuple-element.40), channel_id=1, source_target_pairs={{1,0},{2,1},{3,2},{4,3},{5,4},{6,5},{7,6},{9,8},{10,9},{11,10},{12... | collective-permute-start | bytes 6152 | tf_op jit(solution)/shard_map/ppermute | solution.py:22
  6.9 3.0 %fusion.11 = (bf16[512,2,2,128]{3,2,1,0:T(2,128)(2,1)S(1)}, bf16[512,2,2,128]{3,2,1,0:T(2,128)(2,1)S(1)}) fusion(bf16[512,2,16,128]{3,2,1,0:T(8,128)(2,1)} %param.2), kind=kLoop, calls=%fused_computation.39 | loop fusion | bytes 2097152 | tf_op jit(solution)/shard_map/slice | solution.py:147
  10.0 0.7 copy.8
  10.7 0.2 copy.5
  10.9 1.9 %collective-permute-start = (bf16[512,512]{1,0:T(8,128)(2,1)S(1)}, bf16[512,512]{1,0:T(8,128)(2,1)S(1)}, u32[]{:S(2)}, u32[]{:S(2)}) collective-permute-start(bf16[512,512]{1,0:T(8,128)(2,1)S(1)} %copy.5), channel_id=1, source_target_pairs={{0,1},{1,2},{2,3},{3,4},{4,5},{5,6},{6,7},{8,9},{9,10},{10,11},{11... | collective-permute-start | bytes 1572872 | tf_op jit(solution)/shard_map/ppermute | solution.py:131
  12.9 0.7 copy.9
  13.8 3.6 %collective-permute-start.1 = (bf16[512,512]{1,0:T(8,128)(2,1)S(1)}, bf16[512,512]{1,0:T(8,128)(2,1)S(1)}, u32[]{:S(2)}, u32[]{:S(2)}) collective-permute-start(bf16[512,512]{1,0:T(8,128)(2,1)S(1)} %copy.7), channel_id=1, source_target_pairs={{1,0},{2,1},{3,2},{4,3},{5,4},{6,5},{7,6},{9,8},{10,9},{11,10},{12... | collective-permute-start | bytes 1572872 | tf_op jit(solution)/shard_map/ppermute | solution.py:132
  17.6 8.4 %copy.13 = bf16[64,8,32,128]{3,1,2,0:T(8,128)(2,1)} copy(bf16[64,8,32,128]{3,2,1,0:T(8,128)(2,1)} %bitcast.18) | data formatting | bytes 8388608
  26.3 0.7 broadcast_select_fusion.refs_3_
  27.1 0.8 copy-done.2
  28.0 18.3 %two_steps.2 = (bf16[512,4096]{1,0:T(8,128)(2,1)}, bf16[512,2048]{1,0:T(8,128)(2,1)}, bf16[512,2048]{1,0:T(8,128)(2,1)}) custom-call(bf16[512,4096]{1,0:T(8,128)(2,1)} %bitcast.16, bf16[512,512]{1,0:T(8,128)(2,1)} %copy-done.2, bf16[512,512]{1,0:T(8,128)(2,1)} %copy-done.3, f32[6,36,128]{2,1,0:T(8,128)} %broadcast_select_fusion.refs_3_), custom_call_target="tpu_custom_call" | custom-call | flops 50331648 | bytes 16777216 | tf_op jit(solution)/shard_map/two_steps/pallas_call | solution.py:110
  46.4 4.8 %collective-permute-start.5 = (bf16[512,2048]{1,0:T(8,128)(2,1)}, bf16[512,2048]{1,0:T(8,128)(2,1)}, u32[]{:S(2)}, u32[]{:S(2)}) collective-permute-start(bf16[512,2048]{1,0:T(8,128)(2,1)} %get-tuple-element.15), channel_id=1, source_target_pairs={{0,8},{24,16},{1,9},{25,17},{2,10},{26,18},{3,11},{27,19},{4,12},{... | collective-permute-start | bytes 6291464 | tf_op jit(solution)/shard_map/ppermute | solution.py:390
  51.2 1.4 fusion.10
  52.6 1.9 %collective-permute-start.6 = (bf16[512,512]{1,0:T(8,128)(2,1)S(1)}, bf16[512,512]{1,0:T(8,128)(2,1)S(1)}, u32[]{:S(2)}, u32[]{:S(2)}) collective-permute-start(bf16[512,512]{1,0:T(8,128)(2,1)S(1)} %pad_maximum_fusion), channel_id=1, source_target_pairs={{0,1},{1,2},{2,3},{3,4},{4,5},{5,6},{6,7},{8,9},{9,10},{10,11},{11... | collective-permute-start | bytes 1572872 | tf_op jit(solution)/shard_map/ppermute | solution.py:131
  54.6 3.6 %collective-permute-start.7 = (bf16[512,512]{1,0:T(8,128)(2,1)S(1)}, bf16[512,512]{1,0:T(8,128)(2,1)S(1)}, u32[]{:S(2)}, u32[]{:S(2)}) collective-permute-start(bf16[512,512]{1,0:T(8,128)(2,1)S(1)} %pad_maximum_fusion.1), channel_id=1, source_target_pairs={{1,0},{2,1},{3,2},{4,3},{5,4},{6,5},{7,6},{9,8},{10,9},{11,10},{12... | collective-permute-start | bytes 1572872 | tf_op jit(solution)/shard_map/ppermute | solution.py:132
  58.3 2.0 %collective-permute-start.9 = (bf16[512,2048]{1,0:T(8,128)(2,1)}, bf16[512,2048]{1,0:T(8,128)(2,1)}, u32[]{:S(2)}, u32[]{:S(2)}) collective-permute-start(bf16[512,2048]{1,0:T(8,128)(2,1)} %get-tuple-element.15), channel_id=1, source_target_pairs={{8,16},{16,8},{9,17},{17,9},{10,18},{18,10},{11,19},{19,11},{12,20... | collective-permute-start | bytes 6291464 | tf_op jit(solution)/shard_map/ppermute | solution.py:389
  60.3 2.9 %collective-permute-start.4 = (bf16[512,2048]{1,0:T(8,128)(2,1)S(1)}, bf16[512,2048]{1,0:T(8,128)(2,1)}, u32[]{:S(2)}, u32[]{:S(2)}) collective-permute-start(bf16[512,2048]{1,0:T(8,128)(2,1)S(1)} %copy-done), channel_id=1, source_target_pairs={{0,8},{24,16},{1,9},{25,17},{2,10},{26,18},{3,11},{27,19},{4,12},{... | collective-permute-start | bytes 6291464 | tf_op jit(solution)/shard_map/ppermute | solution.py:391
  63.2 1.7 collective-permute-done.7.refs_2_
  64.9 0.8 copy-done.5
  65.7 17.4 %two_steps.3 = bf16[512,4096]{1,0:T(8,128)(2,1)} custom-call(bf16[512,4096]{1,0:T(8,128)(2,1)} %get-tuple-element.16.refs_0_, bf16[512,512]{1,0:T(8,128)(2,1)} %copy-done.4, bf16[512,512]{1,0:T(8,128)(2,1)} %copy-done.5, f32[6,36,128]{2,1,0:T(8,128)} %broadcast_select_fusion.refs_3_), custom_call_target="tpu_custom_call" | custom-call | flops 50331648 | bytes 16777216 | tf_op jit(solution)/shard_map/two_steps/pallas_call | solution.py:110
  83.1 5.6 %copy.11 = bf16[64,8,32,128]{3,2,1,0:T(8,128)(2,1)} copy(bf16[64,8,32,128]{3,1,2,0:T(8,128)(2,1)} %bitcast.17) | data formatting | bytes 8388608
  88.7 7.5 %collective-permute-done.5 = bf16[512,2048]{1,0:T(8,128)(2,1)} collective-permute-done((bf16[512,2048]{1,0:T(8,128)(2,1)}, bf16[512,2048]{1,0:T(8,128)(2,1)}, u32[]{:S(2)}, u32[]{:S(2)}) %collective-permute-start.5) | collective-permute-done | bytes 2097184 | tf_op jit(solution)/shard_map/ppermute | solution.py:390
  96.2 1.0 collective-permute-start.8
  97.2 2.4 %convolution_convert_fusion.refs_0_ = bf16[512,512]{1,0:T(8,128)(2,1)S(1)} fusion(bf16[512,4096]{1,0:T(8,128)(2,1)S(1)} %copy-done.1), kind=kOutput, calls=%fused_computation.1 | convolution fusion | flops 2147745792 | bytes 4718592 | tf_op jit(solution)/shard_map/dot_general | solution.py:383
  99.6 15.9 %place_early.1.refs_6_ = f32[512,256]{1,0:T(8,128)S(1)} custom-call(bf16[512,512]{1,0:T(8,128)(2,1)S(1)} %convolution_convert_fusion.refs_0_), custom_call_target="tpu_custom_call" | custom-call | bytes 50000000 | tf_op jit(solution)/shard_map/place_early/pallas_call | solution.py:350
  115.4 3.5 %fusion.13.refs_4_ = f32[512,512]{1,0:T(8,128)S(1)} fusion(bf16[512,2048]{1,0:T(8,128)(2,1)} %collective-permute-done.5, bf16[512,2048]{1,0:T(8,128)(2,1)} %get-tuple-element.15), kind=kOutput, calls=%fused_computation.41 | convolution fusion | flops 1073741824 | bytes 5242880 | tf_op jit(solution)/shard_map/dot_general | solution.py:383
  119.0 2.9 %convolution_convert_fusion.1.refs_5_ = bf16[512,512]{1,0:T(8,128)(2,1)S(1)} fusion(bf16[512,2048]{1,0:T(8,128)(2,1)S(1)} %copy-done, bf16[512,2048]{1,0:T(8,128)(2,1)} %collective-permute-done.9.refs_1_), kind=kOutput, calls=%fused_computation.2 | convolution fusion | flops 1074003968 | bytes 4718592 | tf_op jit(solution)/shard_map/dot_general | solution.py:383
  121.8 16.9 %collective-permute-done.4.refs_0_ = bf16[512,2048]{1,0:T(8,128)(2,1)} collective-permute-done((bf16[512,2048]{1,0:T(8,128)(2,1)S(1)}, bf16[512,2048]{1,0:T(8,128)(2,1)}, u32[]{:S(2)}, u32[]{:S(2)}) %collective-permute-start.4) | collective-permute-done | bytes 2097184 | tf_op jit(solution)/shard_map/ppermute | solution.py:391
  138.8 47.3 %place_late.1 = f32[512,256]{1,0:T(8,128)S(1)} custom-call(bf16[512,2048]{1,0:T(8,128)(2,1)} %collective-permute-done.4.refs_0_, bf16[512,2048]{1,0:T(8,128)(2,1)} %collective-permute-done.9.refs_1_, bf16[512,2048]{1,0:T(8,128)(2,1)S(1)} %collective-permute-done.8.refs_2_, bf16[512,2048]{1,0:T(8,128)(2,1)S(1)} %copy-done, f32[512,512]{1,0:T(8,128)S(1)} %fusion.13.refs_4_, ...), custom_call_target="tpu_custom_call" | custom-call | bytes 50000000 | tf_op jit(solution)/shard_map/place_late/pallas_call | solution.py:350
  186.1 0.8 copy.20
  (41 shorter events, 0.8 us)
Async XLA Ops:
  1.4 24.7 %collective-permute-start.2 = (f32[2,2,128]{2,1,0:T(2,128)S(1)}, f32[2,2,128]{2,1,0:T(2,128)S(1)}, u32[]{:S(2)}, u32[]{:S(2)}) collective-permute-start(f32[2,2,128]{2,1,0:T(2,128)S(1)} %get-tuple-element.39), channel_id=1, source_target_pairs={{0,1},{1,2},{2,3},{3,4},{4,5},{5,6},{6,7},{8,9},{9,10},{10,11},{11... | collective-permute-start | bytes 6152 | tf_op jit(solution)/shard_map/ppermute | solution.py:19
  3.3 22.8 %collective-permute-start.3 = (f32[2,2,128]{2,1,0:T(2,128)S(1)}, f32[2,2,128]{2,1,0:T(2,128)S(1)}, u32[]{:S(2)}, u32[]{:S(2)}) collective-permute-start(f32[2,2,128]{2,1,0:T(2,128)S(1)} %get-tuple-element.40), channel_id=1, source_target_pairs={{1,0},{2,1},{3,2},{4,3},{5,4},{6,5},{7,6},{9,8},{10,9},{11,10},{12... | collective-permute-start | bytes 6152 | tf_op jit(solution)/shard_map/ppermute | solution.py:22
  10.9 16.2 %collective-permute-start = (bf16[512,512]{1,0:T(8,128)(2,1)S(1)}, bf16[512,512]{1,0:T(8,128)(2,1)S(1)}, u32[]{:S(2)}, u32[]{:S(2)}) collective-permute-start(bf16[512,512]{1,0:T(8,128)(2,1)S(1)} %copy.5), channel_id=1, source_target_pairs={{0,1},{1,2},{2,3},{3,4},{4,5},{5,6},{6,7},{8,9},{9,10},{10,11},{11... | collective-permute-start | bytes 1572872 | tf_op jit(solution)/shard_map/ppermute | solution.py:131
  13.8 13.3 %collective-permute-start.1 = (bf16[512,512]{1,0:T(8,128)(2,1)S(1)}, bf16[512,512]{1,0:T(8,128)(2,1)S(1)}, u32[]{:S(2)}, u32[]{:S(2)}) collective-permute-start(bf16[512,512]{1,0:T(8,128)(2,1)S(1)} %copy.7), channel_id=1, source_target_pairs={{1,0},{2,1},{3,2},{4,3},{5,4},{6,5},{7,6},{9,8},{10,9},{11,10},{12... | collective-permute-start | bytes 1572872 | tf_op jit(solution)/shard_map/ppermute | solution.py:132
  17.6 8.5 %copy-start.6 = (f32[2,16,128]{2,1,0:T(8,128)S(1)}, f32[2,16,128]{2,1,0:T(8,128)}, u32[]{:S(2)}) copy-start(f32[2,16,128]{2,1,0:T(8,128)} %param.3) | copy-start | bytes 49156
  27.1 0.8 copy-start.2
  27.1 1.0 copy-start.3
  46.4 49.9 %collective-permute-start.5 = (bf16[512,2048]{1,0:T(8,128)(2,1)}, bf16[512,2048]{1,0:T(8,128)(2,1)}, u32[]{:S(2)}, u32[]{:S(2)}) collective-permute-start(bf16[512,2048]{1,0:T(8,128)(2,1)} %get-tuple-element.15), channel_id=1, source_target_pairs={{0,8},{24,16},{1,9},{25,17},{2,10},{26,18},{3,11},{27,19},{4,12},{... | collective-permute-start | bytes 6291464 | tf_op jit(solution)/shard_map/ppermute | solution.py:390
  51.2 9.1 %copy-start = (bf16[512,2048]{1,0:T(8,128)(2,1)S(1)}, bf16[512,2048]{1,0:T(8,128)(2,1)}, u32[]{:S(2)}) copy-start(bf16[512,2048]{1,0:T(8,128)(2,1)} %get-tuple-element.14.refs_3_) | copy-start | bytes 6291460
  52.6 10.6 %collective-permute-start.6 = (bf16[512,512]{1,0:T(8,128)(2,1)S(1)}, bf16[512,512]{1,0:T(8,128)(2,1)S(1)}, u32[]{:S(2)}, u32[]{:S(2)}) collective-permute-start(bf16[512,512]{1,0:T(8,128)(2,1)S(1)} %pad_maximum_fusion), channel_id=1, source_target_pairs={{0,1},{1,2},{2,3},{3,4},{4,5},{5,6},{6,7},{8,9},{9,10},{10,11},{11... | collective-permute-start | bytes 1572872 | tf_op jit(solution)/shard_map/ppermute | solution.py:131
  54.6 10.3 %collective-permute-start.7 = (bf16[512,512]{1,0:T(8,128)(2,1)S(1)}, bf16[512,512]{1,0:T(8,128)(2,1)S(1)}, u32[]{:S(2)}, u32[]{:S(2)}) collective-permute-start(bf16[512,512]{1,0:T(8,128)(2,1)S(1)} %pad_maximum_fusion.1), channel_id=1, source_target_pairs={{1,0},{2,1},{3,2},{4,3},{5,4},{6,5},{7,6},{9,8},{10,9},{11,10},{12... | collective-permute-start | bytes 1572872 | tf_op jit(solution)/shard_map/ppermute | solution.py:132
  58.3 60.7 %collective-permute-start.9 = (bf16[512,2048]{1,0:T(8,128)(2,1)}, bf16[512,2048]{1,0:T(8,128)(2,1)}, u32[]{:S(2)}, u32[]{:S(2)}) collective-permute-start(bf16[512,2048]{1,0:T(8,128)(2,1)} %get-tuple-element.15), channel_id=1, source_target_pairs={{8,16},{16,8},{9,17},{17,9},{10,18},{18,10},{11,19},{19,11},{12,20... | collective-permute-start | bytes 6291464 | tf_op jit(solution)/shard_map/ppermute | solution.py:389
  60.3 78.5 %collective-permute-start.4 = (bf16[512,2048]{1,0:T(8,128)(2,1)S(1)}, bf16[512,2048]{1,0:T(8,128)(2,1)}, u32[]{:S(2)}, u32[]{:S(2)}) collective-permute-start(bf16[512,2048]{1,0:T(8,128)(2,1)S(1)} %copy-done), channel_id=1, source_target_pairs={{0,8},{24,16},{1,9},{25,17},{2,10},{26,18},{3,11},{27,19},{4,12},{... | collective-permute-start | bytes 6291464 | tf_op jit(solution)/shard_map/ppermute | solution.py:391
  63.2 1.7 copy-start.4
  64.9 0.8 copy-start.5
  83.1 14.1 %copy-start.1 = (bf16[512,4096]{1,0:T(8,128)(2,1)S(1)}, bf16[512,4096]{1,0:T(8,128)(2,1)}, u32[]{:S(2)}) copy-start(bf16[512,4096]{1,0:T(8,128)(2,1)} %get-tuple-element.16.refs_0_) | copy-start | bytes 12582916
  96.2 42.6 %collective-permute-start.8 = (bf16[512,2048]{1,0:T(8,128)(2,1)}, bf16[512,2048]{1,0:T(8,128)(2,1)S(1)}, u32[]{:S(2)}, u32[]{:S(2)}) collective-permute-start(bf16[512,2048]{1,0:T(8,128)(2,1)} %collective-permute-done.5), channel_id=1, source_target_pairs={{8,16},{16,8},{9,17},{17,9},{10,18},{18,10},{11,19},{19,11},{12,20... | collective-permute-start | bytes 6291464 | tf_op jit(solution)/shard_map/ppermute | solution.py:393
